TPU v7x, 512 devices: a whole 4x4x16 slice. The times are simulated.
512 devices in a mesh: dp: 256 (over x, y, z), mp: 2 (over core).
Axes of the slice: x: 4, y: 4, z: 16, core: 2. Of those that a mesh axis runs over, the one named last changes fastest.
Arguments:
- embeddings: bfloat16 [786432, 1024], P('dp', 'mp'), may hold values from -24 to 24
- first_level: int32 [786432], P('dp'), may hold values from 0 to 16383, as said below
- second_level: int32 [16384, 1], P('dp'), may hold values from 0 to 1023
Outputs:
- first_centroids: bfloat16 [16384, 1024], P('dp', 'mp')
- second_centroids: bfloat16 [1024, 1024], P('dp', 'mp')
- scores: float32 [16384, 1024], P('dp', 'mp')
Inputs may be any that keep to these rules, and one draw needn't show every extreme that they name: `first_level`: the rows i * 3072 to (i + 1) * 3072 - 1 are assigned only to level-one centroids numbered from ((i + j) mod 256) * 64, that is to the centroids (i + j) * 64 to (i + j + 1) * 64 - 1 taken modulo 16384, for j from 0 to 7; every level-one centroid has at least one row. `second_level`: every level-two centroid is named by at least one level-one centroid.
All inputs are finite; a program needn't handle non-finite values.
Results may differ from a plain program's by a relative error of at most 0.012.
Values may be sent and summed in bfloat16 or wider, within the bound.
A program may use at most 64 MiB of HBM per device.

v0:
```python
import jax
import jax.numpy as jnp
from jax import lax
from jax.sharding import Mesh
from jax.sharding import PartitionSpec as P

CENT_DEV = 64
BAND = 8
K2 = 1024
DP = ("dp_0", "dp_1", "dp_2")


def shifted(value, axis, steps):
    count = lax.axis_size(axis)
    pairs = [(source, (source + steps) % count) for source in range(count)]
    return lax.ppermute(value, axis, pairs)


def in_blocks(array, dim, count):
    dims = array.shape
    tiles = array.reshape(*dims[:dim], count, dims[dim] // count, *dims[dim + 1 :])
    return jnp.moveaxis(tiles, dim, 0)


def summed_on_arrival(array, axis, dim):
    tiles = in_blocks(array, dim, lax.axis_size(axis))
    arrived = lax.all_to_all(tiles, axis, split_axis=0, concat_axis=0, tiled=True)
    return arrived.sum(axis=0)


def sum_by_axis(array, axes, dim):
    far, near = axes
    own = summed_on_arrival(in_blocks(array, dim, lax.axis_size(far)), near, dim + 1)
    return jnp.sum(lax.all_to_all(own, far, 0, 0, tiled=True), axis=0)


def padded_to(lines, count):
    spare = -lines.shape[0] % count
    if not spare:
        return lines
    return jnp.concatenate([lines, jnp.zeros((spare, *lines.shape[1:]), lines.dtype)])


def from_everyone(array, axis):
    copies = jnp.broadcast_to(array, (lax.axis_size(axis), *array.shape))
    return lax.all_to_all(copies, axis, split_axis=0, concat_axis=0, tiled=True)


def laid_out(tiles, dim):
    dims = list(tiles.shape[1:])
    dims[dim] *= tiles.shape[0]
    return jnp.moveaxis(tiles, 0, dim).reshape(dims)


def gather_axes(array, axes, dim):
    far, near = axes
    leading = from_everyone(array, far)
    tiles = jnp.swapaxes(from_everyone(leading, near), 0, 1)
    return laid_out(tiles.reshape(-1, *array.shape), dim)


def total_of(array, axes):
    own = sum_by_axis(padded_to(array, lax.axis_size(axes[0]) * lax.axis_size(axes[1])), axes, 0)
    whole = gather_axes(own, axes, 0)
    return whole[: len(array)].reshape(array.shape)


def in_one(arrays, axis):
    line, at, outs = (jnp.concatenate([a.reshape(-1) for a in arrays]), 0, [])
    so_far = total_of(line, axis)
    for a in arrays:
        outs.append(so_far[at : at + a.size].reshape(a.shape))
        at += a.size
    return tuple(outs)


def sum_at_owner(array, axis, dim):
    count = lax.axis_size(axis)
    tiles = lax.all_to_all(in_blocks(array, dim, count), axis, 0, 0, tiled=True)
    return jnp.sum(tiles.astype(jnp.float32), axis=0)


def shards(embeddings, first_level, second_level):
    devices = lax.axis_size(DP)
    position = lax.axis_index(DP)
    half_width = embeddings.shape[1]
    band_width = BAND * CENT_DEV
    local_ids = (first_level - position * CENT_DEV) % (CENT_DEV * devices)
    block_rows = min(1024, embeddings.shape[0])
    blocks = embeddings.shape[0] // block_rows
    columns = jnp.arange(band_width, dtype=jnp.int32)

    def accumulate(running, pair):
        rows_block, ids_block = pair
        one_hot = (ids_block[:, None] == columns[None, :]).astype(jnp.bfloat16)
        totals = running[0] + jnp.einsum(
            "rk,rd->kd", one_hot, rows_block, preferred_element_type=jnp.float32
        )
        tallies = running[1] + jnp.sum(one_hot.astype(jnp.float32), axis=0)
        return ((totals, tallies), None)

    start_state = (
        jnp.zeros((band_width, half_width), jnp.float32),
        jnp.zeros((band_width,), jnp.float32),
    )
    (totals, tallies), unused = lax.scan(
        accumulate,
        start_state,
        (embeddings.reshape(blocks, block_rows, half_width), local_ids.reshape(blocks, block_rows)),
    )
    totals = totals.reshape(BAND, CENT_DEV, half_width)
    tallies = tallies.reshape(BAND, CENT_DEV)
    summed = totals
    counted = tallies
    for level in range(BAND.bit_length() - 1):
        extent = BAND >> level + 1
        moved = (
            shifted(summed[extent:].astype(jnp.bfloat16), DP, extent).astype(jnp.float32),
            shifted(counted[extent:].astype(jnp.bfloat16), DP, extent).astype(jnp.float32),
        )
        summed = summed[:extent] + moved[0]
        counted = counted[:extent] + moved[1]
    summed = summed[0]
    counted = counted[0]
    first_centroids = (summed / counted[:, None]).astype(jnp.bfloat16)
    second_ids = jnp.arange(K2, dtype=jnp.int32)
    group_hot = (second_level == second_ids[None, :]).astype(jnp.bfloat16)
    group_totals = jnp.einsum(
        "ck,cd->kd", group_hot, first_centroids, preferred_element_type=jnp.float32
    )
    group_counts = jnp.sum(group_hot.astype(jnp.float32), axis=0)
    whole, whole_counts = in_one((group_totals, group_counts), ("dp_0", ("dp_1", "dp_2")))
    every_centroid = (whole / whole_counts[:, None]).astype(jnp.bfloat16)
    owned_rows = K2 // devices
    second_centroids = lax.dynamic_slice_in_dim(
        every_centroid, position * owned_rows, owned_rows, 0
    )
    values = every_centroid.astype(jnp.float32)
    products = jnp.einsum(
        "cd,kd->ck", first_centroids, every_centroid, preferred_element_type=jnp.float32
    )
    partial_value = products - 0.5 * jnp.sum(values * values, axis=1)[None, :]
    scores = sum_at_owner(partial_value.astype(jnp.bfloat16), "mp", 1)
    return (first_centroids, second_centroids, scores)


def solution(mesh):
    torus = Mesh(mesh.devices.reshape(4, 4, 16, mesh.shape["mp"]), ("dp_0", "dp_1", "dp_2", "mp"))
    return jax.shard_map(
        shards,
        mesh=torus,
        in_specs=(P(DP, "mp"), P(DP), P(DP, None)),
        out_specs=(P(DP, "mp"), P(DP, "mp"), P(DP, "mp")),
        check_vma=False,
    )
```

profile of v0, /device:TPU:1, one launch (start us, length us, event | category | flops | bytes accessed | tf_op | source)
XLA Modules:
  0.0 334.0 jit_solution(13225565184118342341)
XLA Ops:
  0.7 0.7 add_select_fusion
  1.4 7.9 %while.13 = (s32[]{:T(128)}, f32[512,512]{1,0:T(8,128)S(1)}, f32[512]{0:T(512)S(1)}, s32[3,1024]{1,0:T(4,128)S(1)}, bf16[3,1024,512]{2,1,0:T(8,128)(2,1)}, /*index=5*/s32[]{:T(128)}, s32[]{:T(128)}) while((s32[]{:T(128)}, f32[512,512]{1,0:T(8,128)S(1)}, f32[512]{0:T(512)S(1)}, s32[3,1024]{1,0:T(4,128)S(1)}, ...), condition=%wide.region_2.3_spmd.clone, body=%wide.region_0.2_spmd.clone.sunk | while | flops 540017152 | bytes 3170408 | solution.py:106
  1.7 2.3 fusion.26
  4.4 2.3 fusion.26
  7.0 2.3 fusion.26
  9.5 9.6 %collective-permute-start.3 = (bf16[4,64]{1,0:T(4,128)(2,1)S(1)}, bf16[4,64]{1,0:T(4,128)(2,1)S(1)}, u32[]{:S(2)}, u32[]{:S(2)}) collective-permute-start(bf16[4,64]{1,0:T(4,128)(2,1)S(1)} %convert_element_type.61), channel_id=1, source_target_pairs={{0,8},{2,10},{4,12},{6,14},{8,16},{10,18},{12,20},{14,22},{16,24},... | collective-permute-start | bytes 1544 | tf_op jit(solution)/shard_map/ppermute | solution.py:16
  19.1 8.8 %collective-permute-start = (bf16[4,64,512]{2,1,0:T(8,128)(2,1)S(1)}, bf16[4,64,512]{2,1,0:T(8,128)(2,1)S(1)}, u32[]{:S(2)}, u32[]{:S(2)}) collective-permute-start(bf16[4,64,512]{2,1,0:T(8,128)(2,1)S(1)} %bitcast.44), channel_id=1, source_target_pairs={{0,8},{2,10},{4,12},{6,14},{8,16},{10,18},{12,20},{14,22},{16,24},... | collective-permute-start | bytes 786440 | tf_op jit(solution)/shard_map/ppermute | solution.py:16
  28.3 3.1 collective-permute-start.4
  31.4 6.1 %collective-permute-done = bf16[4,64,512]{2,1,0:T(8,128)(2,1)S(1)} collective-permute-done((bf16[4,64,512]{2,1,0:T(8,128)(2,1)S(1)}, bf16[4,64,512]{2,1,0:T(8,128)(2,1)S(1)}, u32[]{:S(2)}, u32[]{:S(2)}) %collective-permute-start) | collective-permute-done | bytes 262176 | tf_op jit(solution)/shard_map/ppermute | solution.py:16
  37.7 17.5 %collective-permute-start.1 = (bf16[2,64,512]{2,1,0:T(8,128)(2,1)S(1)}, bf16[2,64,512]{2,1,0:T(8,128)(2,1)S(1)}, u32[]{:S(2)}, u32[]{:S(2)}) collective-permute-start(bf16[2,64,512]{2,1,0:T(8,128)(2,1)S(1)} %slice.116), channel_id=1, source_target_pairs={{0,4},{2,6},{4,8},{6,10},{8,12},{10,14},{12,16},{14,18},{16,20},{1... | collective-permute-start | bytes 393224 | tf_op jit(solution)/shard_map/ppermute | solution.py:16
  55.2 6.3 %collective-permute-start.5 = (bf16[1,64]{1,0:T(2,128)(2,1)S(1)}, bf16[1,64]{1,0:T(2,128)(2,1)S(1)}, u32[]{:S(2)}, u32[]{:S(2)}) collective-permute-start(bf16[1,64]{1,0:T(2,128)(2,1)S(1)} %slice.88), channel_id=1, source_target_pairs={{0,2},{2,4},{4,6},{6,8},{8,10},{10,12},{12,14},{14,16},{16,18},{18... | collective-permute-start | bytes 392 | tf_op jit(solution)/shard_map/ppermute | solution.py:16
  61.6 4.2 %collective-permute-start.2 = (bf16[1,64,512]{2,1,0:T(8,128)(2,1)S(1)}, bf16[1,64,512]{2,1,0:T(8,128)(2,1)S(1)}, u32[]{:S(2)}, u32[]{:S(2)}) collective-permute-start(bf16[1,64,512]{2,1,0:T(8,128)(2,1)S(1)} %slice.117), channel_id=1, source_target_pairs={{0,2},{2,4},{4,6},{6,8},{8,10},{10,12},{12,14},{14,16},{16,18},{18... | collective-permute-start | bytes 196616 | tf_op jit(solution)/shard_map/ppermute | solution.py:16
  65.8 6.2 %collective-permute-done.2 = bf16[1,64,512]{2,1,0:T(8,128)(2,1)S(1)} collective-permute-done((bf16[1,64,512]{2,1,0:T(8,128)(2,1)S(1)}, bf16[1,64,512]{2,1,0:T(8,128)(2,1)S(1)}, u32[]{:S(2)}, u32[]{:S(2)}) %collective-permute-start.2) | collective-permute-done | bytes 65568 | tf_op jit(solution)/shard_map/ppermute | solution.py:16
  72.1 0.6 convolution_bitcast_fusion
  72.7 0.5 copy.17
  73.2 1.5 pad_maximum_fusion
  74.7 3.1 reshape_reshape.6
  77.8 1.4 copy.11
  79.3 105.6 %all_to_all.33 = f32[64,4,2052]{2,1,0:T(4,128)S(1)} all-to-all(f32[64,4,2052]{2,1,0:T(4,128)S(1)} %copy.11), channel_id=1, replica_groups=mesh['dp_0'=4,'dp_1'=4,'dp_2'=16,'mp'=2] {'dp_1','dp_2'}, dimensions={0} | all-to-all | bytes 4202496 | tf_op jit(solution)/shard_map/all_to_all | solution.py:27
  185.3 10.9 %all_to_all.34 = f32[4,1,2052]{2,1,0:T(1,128)S(1)} all-to-all(f32[4,1,2052]{2,1,0:T(1,128)S(1)} %all_to_all.22), channel_id=1, replica_groups=mesh['dp_0'=4,'dp_1'=4,'dp_2'=16,'mp'=2] {'dp_0'}, dimensions={0} | all-to-all | bytes 65664 | tf_op jit(solution)/shard_map/all_to_all | solution.py:34
  196.3 6.7 %all_to_all.35 = f32[4,1,2052]{2,1,0:T(1,128)S(1)} all-to-all(f32[4,1,2052]{2,1,0:T(1,128)S(1)} %broadcast_in_dim.19), channel_id=1, replica_groups=mesh['dp_0'=4,'dp_1'=4,'dp_2'=16,'mp'=2] {'dp_0'}, dimensions={0} | all-to-all | bytes 65664 | tf_op jit(solution)/shard_map/all_to_all | solution.py:46
  203.0 1.7 broadcast_in_dim.20
  204.6 7.9 %all-to-all-start.3 = ((f32[64,4,2052]{2,1,0:T(4,128)}), f32[64,4,2052]{2,1,0:T(4,128)S(1)}, u32[]{:S(2)}, u32[]{:S(2)}) async-start(f32[64,4,2052]{2,1,0:T(4,128)} %broadcast_in_dim.20), calls=%async_computation.3 | async-start | bytes 4456448 | tf_op jit(solution)/shard_map/all_to_all | solution.py:46
  212.5 96.8 %all-to-all-done.3 = f32[64,4,2052]{2,1,0:T(4,128)S(1)} async-done(((f32[64,4,2052]{2,1,0:T(4,128)}), f32[64,4,2052]{2,1,0:T(4,128)S(1)}, u32[]{:S(2)}, u32[]{:S(2)}) %all-to-all-start.3) | async-done | bytes 2101280 | tf_op jit(solution)/shard_map/all_to_all | solution.py:46
  309.3 1.4 copy-done
  310.7 1.8 copy.12
  312.5 2.9 reshape_reshape.7
  315.4 3.6 %slice.89 = f32[1026,512]{1,0:T(8,128)} reshape(f32[4,64,2052]{2,1,0:T(8,128)S(1)} %copy.12) | data formatting | bytes 4202496 | tf_op jit(solution)/shard_map/slice | solution.py:72
  319.0 2.0 multiply_reduce_fusion
  321.0 0.6 constant_dynamic-slice_fusion.1
  322.1 11.3 %all_to_all.36 = bf16[2,64,512]{2,1,0:T(8,128)(2,1)S(1)} all-to-all(bf16[2,64,512]{2,1,0:T(8,128)(2,1)S(1)} %bitcast.43), channel_id=1, replica_groups=mesh['dp_0'=4,'dp_1'=4,'dp_2'=16,'mp'=2] {'mp'}, dimensions={0} | all-to-all | bytes 262144 | tf_op jit(solution)/shard_map/all_to_all | solution.py:79
  333.4 0.7 convert_reduce_fusion.1
  (49 shorter events, 2.6 us)
Async XLA Ops:
  1.4 26.6 %copy-start.2 = (s32[64,1]{0,1:T(1,128)S(1)}, s32[64,1]{0,1:T(1,128)}, u32[]{:S(2)}) copy-start(s32[64,1]{0,1:T(1,128)} %param.7) | copy-start | bytes 772
  9.5 18.9 %collective-permute-start.3 = (bf16[4,64]{1,0:T(4,128)(2,1)S(1)}, bf16[4,64]{1,0:T(4,128)(2,1)S(1)}, u32[]{:S(2)}, u32[]{:S(2)}) collective-permute-start(bf16[4,64]{1,0:T(4,128)(2,1)S(1)} %convert_element_type.61), channel_id=1, source_target_pairs={{0,8},{2,10},{4,12},{6,14},{8,16},{10,18},{12,20},{14,22},{16,24},... | collective-permute-start | bytes 1544 | tf_op jit(solution)/shard_map/ppermute | solution.py:16
  19.1 18.4 %collective-permute-start = (bf16[4,64,512]{2,1,0:T(8,128)(2,1)S(1)}, bf16[4,64,512]{2,1,0:T(8,128)(2,1)S(1)}, u32[]{:S(2)}, u32[]{:S(2)}) collective-permute-start(bf16[4,64,512]{2,1,0:T(8,128)(2,1)S(1)} %bitcast.44), channel_id=1, source_target_pairs={{0,8},{2,10},{4,12},{6,14},{8,16},{10,18},{12,20},{14,22},{16,24},... | collective-permute-start | bytes 786440 | tf_op jit(solution)/shard_map/ppermute | solution.py:16
  28.3 26.8 %collective-permute-start.4 = (bf16[2,64]{1,0:T(2,128)(2,1)S(1)}, bf16[2,64]{1,0:T(2,128)(2,1)S(1)}, u32[]{:S(2)}, u32[]{:S(2)}) collective-permute-start(bf16[2,64]{1,0:T(2,128)(2,1)S(1)} %slice.86), channel_id=1, source_target_pairs={{0,4},{2,6},{4,8},{6,10},{8,12},{10,14},{12,16},{14,18},{16,20},{1... | collective-permute-start | bytes 776 | tf_op jit(solution)/shard_map/ppermute | solution.py:16
  37.7 23.8 %collective-permute-start.1 = (bf16[2,64,512]{2,1,0:T(8,128)(2,1)S(1)}, bf16[2,64,512]{2,1,0:T(8,128)(2,1)S(1)}, u32[]{:S(2)}, u32[]{:S(2)}) collective-permute-start(bf16[2,64,512]{2,1,0:T(8,128)(2,1)S(1)} %slice.116), channel_id=1, source_target_pairs={{0,4},{2,6},{4,8},{6,10},{8,12},{10,14},{12,16},{14,18},{16,20},{1... | collective-permute-start | bytes 393224 | tf_op jit(solution)/shard_map/ppermute | solution.py:16
  55.2 10.6 %collective-permute-start.5 = (bf16[1,64]{1,0:T(2,128)(2,1)S(1)}, bf16[1,64]{1,0:T(2,128)(2,1)S(1)}, u32[]{:S(2)}, u32[]{:S(2)}) collective-permute-start(bf16[1,64]{1,0:T(2,128)(2,1)S(1)} %slice.88), channel_id=1, source_target_pairs={{0,2},{2,4},{4,6},{6,8},{8,10},{10,12},{12,14},{14,16},{16,18},{18... | collective-permute-start | bytes 392 | tf_op jit(solution)/shard_map/ppermute | solution.py:16
  61.6 10.4 %collective-permute-start.2 = (bf16[1,64,512]{2,1,0:T(8,128)(2,1)S(1)}, bf16[1,64,512]{2,1,0:T(8,128)(2,1)S(1)}, u32[]{:S(2)}, u32[]{:S(2)}) collective-permute-start(bf16[1,64,512]{2,1,0:T(8,128)(2,1)S(1)} %slice.117), channel_id=1, source_target_pairs={{0,2},{2,4},{4,6},{6,8},{8,10},{10,12},{12,14},{14,16},{16,18},{18... | collective-permute-start | bytes 196616 | tf_op jit(solution)/shard_map/ppermute | solution.py:16
  72.1 249.5 %copy-start.1 = (bf16[64,512]{1,0:T(8,128)(2,1)}, bf16[64,512]{1,0:T(8,128)(2,1)S(1)}, u32[]{:S(2)}) copy-start(bf16[64,512]{1,0:T(8,128)(2,1)S(1)} %fusion.14) | copy-start | bytes 196612
  204.6 104.7 %all-to-all-start.3 = ((f32[64,4,2052]{2,1,0:T(4,128)}), f32[64,4,2052]{2,1,0:T(4,128)S(1)}, u32[]{:S(2)}, u32[]{:S(2)}) async-start(f32[64,4,2052]{2,1,0:T(4,128)} %broadcast_in_dim.20), calls=%async_computation.3 | async-start | bytes 4456448 | tf_op jit(solution)/shard_map/all_to_all | solution.py:46
  309.3 1.4 copy-start
  315.4 3.6 %slice-start = ((f32[525312]{0:T(1024)}), f32[1024]{0:T(1024)S(1)}, s32[]{:S(2)}) async-start(f32[525312]{0:T(1024)} %reshape_reshape.7), calls=%async_computation.5 | async-start | bytes 8192 | tf_op jit(solution)/shard_map/slice | solution.py:72
where the time goes:
time: 335 us; the launch traced here: 334 us
  blocking collectives  134 us (40%)
  waiting for transfers between devices  109 us (33%)
  starting transfers between devices  57.4 us (17%)
  local copies, waits for them, and re-layouts  17.5 us (5%)
  matrix products  7.92 us (2%)
  other arithmetic  6.54 us (2%)
    all_to_all x1, blocking collectives, summed_on_arrival(): lax.all_to_all(tiles, axis, split_axis=0, concat_axis=0, tiled=True)  106 us
    all_to_all x1, waiting for transfers between devices, from_everyone(): return lax.all_to_all(copies, axis, split_axis=0, concat_axis=0, tiled=True)  96.8 us
    ppermute x6, starting transfers between devices, shifted(): return lax.ppermute(value, axis, pairs)  49.5 us
    ppermute x6, waiting for transfers between devices, shifted(): return lax.ppermute(value, axis, pairs)  12.4 us
    all_to_all x1, blocking collectives, sum_at_owner(): tiles = lax.all_to_all(in_blocks(array, dim, count), axis, 0, 0, tiled=True)  11.3 us
    all_to_all x1, blocking collectives, sum_by_axis(): return jnp.sum(lax.all_to_all(own, far, 0, 0, tiled=True), axis=0)  10.9 us
    all_to_all x1, starting transfers between devices, from_everyone(): return lax.all_to_all(copies, axis, split_axis=0, concat_axis=0, tiled=True)  7.85 us
    dot_general x3, matrix products, accumulate(): jnp.einsum('rk,rd->kd', one_hot, rows_block, preferred_element_type=jnp.f...  6.93 us
  transfers between devices with their start and end apart: 7, of which 4 were waited for; matrix products, arithmetic and copies ran while one was open for 0% of the time, Pallas kernels for 0%

commit v1 on v0

v1 whole, which is shorter than its diff:
```python
import jax
import jax.numpy as jnp
from jax import lax
from jax.experimental import pallas as pl
from jax.experimental.pallas import tpu as pltpu
from jax.sharding import Mesh
from jax.sharding import PartitionSpec as P

NX, NY, NZ = 4, 4, 16
CENT = 64
BAND = 8
ROWS = 3072
HALF = 512
K1 = 16384
PIECES = 4
PROWS = CENT // PIECES
DP = ("dp_0", "dp_1", "dp_2")
MESH = pl.DeviceIdType.MESH
F32 = jnp.float32
BF16 = jnp.bfloat16


def dot_nt(a, b):
    return lax.dot_general(a, b, (((1,), (1,)), ((), ())), preferred_element_type=F32)


def kernel(
    emb_hbm, ids_ref, sec_ref,
    fc_out, sc_out, scores_out,
    emb, oh, part, csend, crecv, cntpart, cntsend, cntrecv,
    xg, idbuf, oh2, ysend, yrecv, ypart, ycsend, ycrecv, zcsend, zcrecv,
    zsend, zpart, zrecv, zg, bsend, yg, ssend, sret,
    emb_sem, c_ss, c_rs, cc_ss, cc_rs, x_ss, x_rs, id_ss, id_rs, pt_ss, pt_rs,
    y_ss, y_rs, yc_ss, yc_rs, zc_ss, zc_rs, z_ss, z_rs, za_ss, za_rs,
    ya_ss, ya_rs, r_ss, r_rs,
):
    x = lax.axis_index("dp_0")
    y = lax.axis_index("dp_1")
    z = lax.axis_index("dp_2")
    c = lax.axis_index("mp")
    me = (x * NY + y) * NZ + z
    devices = NX * NY * NZ

    def coords(index):
        return (index // (NY * NZ), lax.rem(index // NZ, NY), lax.rem(index, NZ), c)

    after = coords(lax.rem(me + 1, devices))
    before = coords(lax.rem(me + devices - 1, devices))

    def xdev(step, core):
        return (lax.rem(x + step, NX), y, z, core)

    def ydev(step, core):
        return (x, lax.rem(y + step, NY), z, core)

    def zdev(step):
        return (x, y, lax.rem(z + step, NZ), c)

    load = pltpu.make_async_copy(emb_hbm, emb, emb_sem)
    load.start()

    barrier = pltpu.get_barrier_semaphore()
    peers = [after, before, (x, y, z, 1 - c)]
    for step in range(1, NX):
        peers += [xdev(step, 0), xdev(step, 1)]
    for step in range(1, NY):
        peers += [ydev(step, 0), ydev(step, 1)]
    for step in range(1, NZ):
        peers.append(zdev(step))
    for peer in peers:
        pl.semaphore_signal(barrier, inc=1, device_id=peer, device_id_type=MESH)

    pending = []

    def send(src, dst, ssem, rsem, device):
        copy = pltpu.make_async_remote_copy(
            src_ref=src, dst_ref=dst, send_sem=ssem, recv_sem=rsem, device_id=device, device_id_type=MESH
        )
        copy.start()
        pending.append(copy)

    def arrived(dst, ssem, rsem):
        pltpu.make_async_remote_copy(
            src_ref=dst, dst_ref=dst, send_sem=ssem, recv_sem=rsem, device_id=after, device_id_type=MESH
        ).wait_recv()

    shifted = ids_ref[...] - me * CENT
    local = jnp.where(shifted < 0, shifted + K1, shifted)
    ones_row = jnp.ones((8, 128), BF16)

    def one_hot_block(j):
        wanted = lax.broadcasted_iota(jnp.int32, (CENT, ROWS), 0) + j * CENT
        oh[pl.ds(j * CENT, CENT), :] = jnp.where(local == wanted, 1.0, 0.0).astype(BF16)

    def counts_block(j):
        folded = oh[pl.ds(j * CENT, CENT), pl.ds(0, 128)]
        for k in range(1, ROWS // 128):
            folded = folded + oh[pl.ds(j * CENT, CENT), pl.ds(k * 128, 128)]
        cntpart[j, :, pl.ds(0, CENT)] = dot_nt(ones_row, folded)[0:1]

    half = BAND // 2 * CENT
    for j in range(BAND // 2, BAND):
        one_hot_block(j)
    load.wait()
    part[pl.ds(half, half), :] = jnp.dot(oh[pl.ds(half, half), :], emb[...], preferred_element_type=F32)
    cntpart[...] = jnp.zeros_like(cntpart)
    for j in range(BAND // 2, BAND):
        counts_block(j)
    idbuf[x, :, pl.ds(0, CENT)] = sec_ref[...]
    idbuf[x, :, pl.ds(CENT, CENT)] = sec_ref[...]

    pl.semaphore_wait(barrier, len(peers))

    def chain_send(s):
        j = BAND - s
        for p in range(PIECES):
            rows = pl.ds(p * PROWS, PROWS)
            total = part[pl.ds(j * CENT + p * PROWS, PROWS), :]
            if s > 1:
                arrived(crecv.at[s - 2, rows], c_ss.at[s - 2, p], c_rs.at[s - 2, p])
                total = total + crecv[s - 2, rows].astype(F32)
            csend[s - 1, rows] = total.astype(BF16)
            send(csend.at[s - 1, rows], crecv.at[s - 1, rows], c_ss.at[s - 1, p], c_rs.at[s - 1, p], after)
        count = cntpart[j]
        if s > 1:
            arrived(cntrecv.at[s - 2], cc_ss.at[s - 2], cc_rs.at[s - 2])
            count = count + cntrecv[s - 2]
        cntsend[s - 1] = count
        send(cntsend.at[s - 1], cntrecv.at[s - 1], cc_ss.at[s - 1], cc_rs.at[s - 1], after)

    chain_send(1)
    for step in range(1, NX):
        send(idbuf.at[x], idbuf.at[x], id_ss.at[step - 1], id_rs.at[step - 1], xdev(step, c))
    for j in range(BAND // 2):
        one_hot_block(j)
    part[pl.ds(0, half), :] = jnp.dot(oh[pl.ds(0, half), :], emb[...], preferred_element_type=F32)
    for j in range(BAND // 2):
        counts_block(j)
    chain_send(2)

    for step in range(1, NX):
        arrived(idbuf.at[lax.rem(x + NX - step, NX)], id_ss.at[step - 1], id_rs.at[step - 1])
    wide = NY * NZ * 8
    lane = lax.broadcasted_iota(jnp.int32, (1, 128), 1)
    row = lax.broadcasted_iota(jnp.int32, (wide, 128), 0)
    group = x * (NY * NZ * 4) + (row // 8) * 4 + lax.rem(row, 4)
    upper = lax.rem(row, 8) < 4
    for pair in range(NX // 2):
        names = jnp.where(lane < CENT, idbuf[2 * pair], idbuf[2 * pair + 1])
        hit = names == group
        oh2[0, :, pl.ds(pair * 128, 128)] = jnp.where(hit & upper, 1.0, 0.0).astype(BF16)
        oh2[1, :, pl.ds(pair * 128, 128)] = jnp.where(hit & ~upper, 1.0, 0.0).astype(BF16)
    ones_wide = jnp.ones((8, NX * CENT), BF16)
    for k in range(NY):
        rows = pl.ds(k * NZ * 8, NZ * 8)
        ycsend[k] = (dot_nt(ones_wide, oh2[0, rows, :]) + dot_nt(ones_wide, oh2[1, rows, :]))[0:1]
    for step in range(1, NY):
        to = lax.rem(y + step, NY)
        send(ycsend.at[to], ycrecv.at[step - 1], yc_ss.at[step - 1], yc_rs.at[step - 1], ydev(step, c))
    chain_send(3)
    chain_send(4)
    line = ycsend[y]
    for step in range(1, NY):
        arrived(ycrecv.at[step - 1], yc_ss.at[step - 1], yc_rs.at[step - 1])
        line = line + ycrecv[step - 1]
    zcsend[...] = line
    for step in range(1, NZ):
        send(zcsend, zcrecv.at[step - 1], zc_ss.at[step - 1], zc_rs.at[step - 1], zdev(step))
    chain_send(5)
    chain_send(6)
    chain_send(7)

    last = BAND - 2
    arrived(cntrecv.at[last], cc_ss.at[last], cc_rs.at[last])
    count_row = (cntpart[0] + cntrecv[last])[:, 0:CENT]
    eye = lax.broadcasted_iota(jnp.int32, (CENT, CENT), 0) == lax.broadcasted_iota(jnp.int32, (CENT, CENT), 1)
    count_column = jnp.sum(jnp.where(eye, count_row, 0.0), axis=1, keepdims=True)
    for p in range(PIECES):
        rows = pl.ds(p * PROWS, PROWS)
        arrived(crecv.at[last, rows], c_ss.at[last, p], c_rs.at[last, p])
        total = part[rows, :] + crecv[last, rows].astype(F32)
        done = (total / count_column[p * PROWS : (p + 1) * PROWS]).astype(BF16)
        fc_out[rows, :] = done
        xg[c, x, rows] = done
        for step in range(1, NX):
            send(xg.at[c, x, rows], xg.at[c, x, rows], x_ss.at[step - 1, p], x_rs.at[step - 1, p], xdev(step, c))
    for step in range(1, NX):
        source = lax.rem(x + NX - step, NX)
        for p in range(PIECES):
            rows = pl.ds(p * PROWS, PROWS)
            arrived(xg.at[c, source, rows], x_ss.at[step - 1, p], x_rs.at[step - 1, p])
    send(xg.at[c], xg.at[c], pt_ss, pt_rs, (x, y, z, 1 - c))

    mine = xg[c].reshape(NX * CENT, HALF)
    for step in list(range(1, NY)) + [0]:
        to = lax.rem(y + step, NY)
        rows = pl.ds(pl.multiple_of(to * NZ * 8, NZ * 8), NZ * 8)
        sums = jnp.dot(oh2[0, rows, :], mine[:, : HALF // 2], preferred_element_type=F32)
        sums = sums + jnp.dot(oh2[1, rows, :], mine[:, HALF // 2 :], preferred_element_type=F32)
        if step:
            ysend[step - 1] = sums.astype(BF16)
            send(ysend.at[step - 1], yrecv.at[step - 1], y_ss.at[step - 1], y_rs.at[step - 1], ydev(step, c))
        else:
            ypart[...] = sums
    sums = ypart[...]
    for step in range(1, NY):
        arrived(yrecv.at[step - 1], y_ss.at[step - 1], y_rs.at[step - 1])
        sums = sums + yrecv[step - 1].astype(F32)
    zpart[...] = sums.reshape(NZ, 8, HALF // 2)
    zsend[...] = sums.reshape(NZ, 8, HALF // 2).astype(BF16)
    order = sorted(range(1, NZ), key=lambda step: -min(step, NZ - step))
    for step in order:
        to = lax.rem(z + step, NZ)
        send(zsend.at[to], zrecv.at[step - 1], z_ss.at[step - 1], z_rs.at[step - 1], zdev(step))
    counts = zcsend[...]
    for step in range(1, NZ):
        arrived(zcrecv.at[step - 1], zc_ss.at[step - 1], zc_rs.at[step - 1])
        counts = counts + zcrecv[step - 1]
    eight = lax.broadcasted_iota(jnp.int32, (8, 128), 0) + z * 8 == lax.broadcasted_iota(jnp.int32, (8, 128), 1)
    second_counts = jnp.sum(jnp.where(eight, counts, 0.0), axis=1, keepdims=True)
    sums = zpart[z]
    for step in reversed(order):
        arrived(zrecv.at[step - 1], z_ss.at[step - 1], z_rs.at[step - 1])
        sums = sums + zrecv[step - 1].astype(F32)
    second = (sums / second_counts).astype(BF16)
    zg[z] = second
    for step in order:
        send(zg.at[z], zg.at[z], za_ss.at[step - 1], za_rs.at[step - 1], zdev(step))
    second32 = second.astype(F32)
    sc_out[:, pl.ds(0, HALF // 2)] = second32[0:4].astype(BF16)
    sc_out[:, pl.ds(HALF // 2, HALF // 2)] = second32[4:8].astype(BF16)
    for step in reversed(order):
        arrived(zg.at[lax.rem(z + NZ - step, NZ)], za_ss.at[step - 1], za_rs.at[step - 1])

    gathered = zg[...].reshape(NZ * 8, HALF // 2)
    index = lax.broadcasted_iota(jnp.int32, (NZ * 4, NZ * 8), 0)
    column = lax.broadcasted_iota(jnp.int32, (NZ * 4, NZ * 8), 1)
    place = (index // 4) * 8 + lax.rem(index, 4)
    for h in range(2):
        pick = jnp.where(column == place + 4 * h, 1.0, 0.0).astype(BF16)
        picked = jnp.dot(pick, gathered, preferred_element_type=F32).astype(BF16)
        bsend[:, pl.ds(h * (HALF // 2), HALF // 2)] = picked
    scorer = y // (NY // 2)
    slot = lax.rem(y, NY // 2)
    for step in range(1, NY):
        send(bsend, yg.at[c, slot], ya_ss.at[step], ya_rs.at[c, slot], ydev(step, scorer))
    own_scorer = scorer == c

    @pl.when(own_scorer)
    def _():
        yg[c, slot] = bsend[...]

    @pl.when(jnp.logical_not(own_scorer))
    def _():
        pltpu.make_async_remote_copy(
            src_ref=bsend, dst_ref=yg.at[c, slot], send_sem=ya_ss.at[0], recv_sem=ya_rs.at[c, slot],
            device_id=(x, y, z, 1 - c), device_id_type=MESH,
        ).start()

    arrived(xg.at[1 - c], pt_ss, pt_rs)
    for s in range(NY // 2):
        for k in range(2):
            here = jnp.logical_and(c * (NY // 2) + s == y, c == k)

            @pl.when(jnp.logical_not(here))
            def _():
                arrived(yg.at[k, s], ya_ss.at[0], ya_rs.at[k, s])

    groups = NY // 2 * NZ * 4
    scores = jnp.zeros((NX * CENT, groups), F32)
    squares = jnp.zeros((groups, 1), F32)
    for k in range(2):
        b = yg[k].reshape(groups, HALF)
        scores = scores + dot_nt(xg[k].reshape(NX * CENT, HALF), b)
        b32 = b.astype(F32)
        squares = squares + jnp.sum(b32 * b32, axis=1, keepdims=True)
    eye = lax.broadcasted_iota(jnp.int32, (groups, groups), 0) == lax.broadcasted_iota(jnp.int32, (groups, groups), 1)
    norm_row = jnp.sum(jnp.where(eye, squares, 0.0), axis=0, keepdims=True)
    ssend[...] = (scores - 0.5 * norm_row).astype(BF16).reshape(NX, CENT, groups)
    holder = x // (NX // 2)
    out_slot = lax.rem(x, NX // 2) * 2 + c
    for step in range(1, NX):
        to = lax.rem(x + step, NX)
        send(ssend.at[to], sret.at[out_slot], r_ss.at[step], r_rs.at[out_slot], xdev(step, holder))
    own_holder = holder == c

    @pl.when(own_holder)
    def _():
        sret[out_slot] = ssend[x]

    @pl.when(jnp.logical_not(own_holder))
    def _():
        pltpu.make_async_remote_copy(
            src_ref=ssend.at[x], dst_ref=sret.at[out_slot], send_sem=r_ss.at[0], recv_sem=r_rs.at[out_slot],
            device_id=(x, y, z, 1 - c), device_id_type=MESH,
        ).start()

    for s in range(NX):
        here = jnp.logical_and(c * (NX // 2) + s // 2 == x, c == s % 2)

        @pl.when(jnp.logical_not(here))
        def _():
            arrived(sret.at[s], r_ss.at[0], r_rs.at[s])

        scores_out[:, pl.ds(s * groups, groups)] = sret[s].astype(F32)

    for copy in pending:
        copy.wait_send()

    @pl.when(jnp.logical_not(own_scorer))
    def _():
        pltpu.make_async_remote_copy(
            src_ref=bsend, dst_ref=yg.at[c, slot], send_sem=ya_ss.at[0], recv_sem=ya_rs.at[c, slot],
            device_id=(x, y, z, 1 - c), device_id_type=MESH,
        ).wait_send()

    @pl.when(jnp.logical_not(own_holder))
    def _():
        pltpu.make_async_remote_copy(
            src_ref=ssend.at[x], dst_ref=sret.at[out_slot], send_sem=r_ss.at[0], recv_sem=r_rs.at[out_slot],
            device_id=(x, y, z, 1 - c), device_id_type=MESH,
        ).wait_send()


def shards(embeddings, first_level, second_level):
    dma = pltpu.SemaphoreType.DMA
    groups = NY // 2 * NZ * 4
    vmem = pl.BlockSpec(memory_space=pltpu.VMEM)
    return pl.pallas_call(
        kernel,
        out_shape=(
            jax.ShapeDtypeStruct((CENT, HALF), BF16),
            jax.ShapeDtypeStruct((4, HALF), BF16),
            jax.ShapeDtypeStruct((CENT, HALF), F32),
        ),
        in_specs=[pl.BlockSpec(memory_space=pl.ANY), vmem, vmem],
        out_specs=(vmem, vmem, vmem),
        scratch_shapes=[
            pltpu.VMEM((ROWS, HALF), BF16),
            pltpu.VMEM((BAND * CENT, ROWS), BF16),
            pltpu.VMEM((BAND * CENT, HALF), F32),
            pltpu.VMEM((BAND - 1, CENT, HALF), BF16),
            pltpu.VMEM((BAND - 1, CENT, HALF), BF16),
            pltpu.VMEM((BAND, 1, 128), F32),
            pltpu.VMEM((BAND - 1, 1, 128), F32),
            pltpu.VMEM((BAND - 1, 1, 128), F32),
            pltpu.VMEM((2, NX, CENT, HALF), BF16),
            pltpu.VMEM((NX, 1, 128), jnp.int32),
            pltpu.VMEM((2, NY * NZ * 8, NX * CENT), BF16),
            pltpu.VMEM((NY - 1, NZ * 8, HALF // 2), BF16),
            pltpu.VMEM((NY - 1, NZ * 8, HALF // 2), BF16),
            pltpu.VMEM((NZ * 8, HALF // 2), F32),
            pltpu.VMEM((NY, 1, 128), F32),
            pltpu.VMEM((NY - 1, 1, 128), F32),
            pltpu.VMEM((1, 128), F32),
            pltpu.VMEM((NZ - 1, 1, 128), F32),
            pltpu.VMEM((NZ, 8, HALF // 2), BF16),
            pltpu.VMEM((NZ, 8, HALF // 2), F32),
            pltpu.VMEM((NZ - 1, 8, HALF // 2), BF16),
            pltpu.VMEM((NZ, 8, HALF // 2), BF16),
            pltpu.VMEM((NZ * 4, HALF), BF16),
            pltpu.VMEM((2, NY // 2, NZ * 4, HALF), BF16),
            pltpu.VMEM((NX, CENT, groups), BF16),
            pltpu.VMEM((NX, CENT, groups), BF16),
            dma,
            dma((BAND - 1, PIECES)), dma((BAND - 1, PIECES)),
            dma((BAND - 1,)), dma((BAND - 1,)),
            dma((NX - 1, PIECES)), dma((NX - 1, PIECES)),
            dma((NX - 1,)), dma((NX - 1,)),
            dma, dma,
            dma((NY - 1,)), dma((NY - 1,)),
            dma((NY - 1,)), dma((NY - 1,)),
            dma((NZ - 1,)), dma((NZ - 1,)),
            dma((NZ - 1,)), dma((NZ - 1,)),
            dma((NZ - 1,)), dma((NZ - 1,)),
            dma((NY,)), dma((2, NY // 2)),
            dma((NX,)), dma((NX,)),
        ],
        compiler_params=pltpu.CompilerParams(
            collective_id=0, has_side_effects=True, vmem_limit_bytes=48 << 20
        ),
        name="update",
    )(embeddings, first_level.reshape(1, ROWS), second_level.reshape(1, CENT))


def solution(mesh):
    torus = Mesh(mesh.devices.reshape(NX, NY, NZ, mesh.shape["mp"]), (*DP, "mp"))
    return jax.shard_map(
        shards,
        mesh=torus,
        in_specs=(P(DP, "mp"), P(DP), P(DP, None)),
        out_specs=(P(DP, "mp"), P(DP, "mp"), P(DP, "mp")),
        check_vma=False,
    )
```

time: 335 us -> 79.9 us (0.24)
  blocking collectives: 134 us -> 0 us
  waiting for transfers between devices: 109 us -> 0 us
  Pallas kernels: 0 us -> 73.9 us
  starting transfers between devices: 57.4 us -> 0 us
  local copies, waits for them, and re-layouts: 17.5 us -> 5.12 us
  matrix products: 7.92 us -> 0 us
  other arithmetic: 6.54 us -> 0 us
    all_to_all x4 -> x0, blocking collectives: 134 us -> none  [the longest x1 106 us: summed_on_arrival(): lax.all_to_all(tiles, axis, split_axis=0, concat_axis=0, tiled=True)]
    all_to_all x1 -> x0, waiting for transfers between devices: 96.8 us -> none  [from_everyone(): return lax.all_to_all(copies, axis, split_axis=0, concat_axis=0, tiled=True)]
    pallas_call x0 -> x1, Pallas kernels: none -> 73.9 us  [shards(): pl.pallas_call(kernel, out_shape=(jax.ShapeDtypeStruct((CENT, HALF), BF16...]
    ppermute x6 -> x0, starting transfers between devices: 49.5 us -> none  [shifted(): return lax.ppermute(value, axis, pairs)]
    ppermute x6 -> x0, waiting for transfers between devices: 12.4 us -> none  [shifted(): return lax.ppermute(value, axis, pairs)]
    dot_general x5 -> x0, matrix products: 7.92 us -> none  [the longest x3 6.93 us: accumulate(): jnp.einsum('rk,rd->kd', one_hot, rows_block, preferred_element_type=jnp.f...]
    all_to_all x1 -> x0, starting transfers between devices: 7.85 us -> none  [from_everyone(): return lax.all_to_all(copies, axis, split_axis=0, concat_axis=0, tiled=True)]
    another operation x2 -> x0, local copies, waits for them, and re-layouts: 6.07 us -> none  [the longest x1 3.13 us: in_blocks(): array.reshape(*dims[:dim], count, dims[dim] // count, *dims[dim + 1:])]
  transfers between devices with their start and end apart: 7 -> 0, of which waited for: 4 -> 0; matrix products, arithmetic and copies ran while one was open for 0% -> 0% of each run, Pallas kernels for 0% -> 0%
where the time goes in v1:
time: 79.9 us; the launch traced here: 79.7 us
  Pallas kernels  73.9 us (92%)
  local copies, waits for them, and re-layouts  5.12 us (6%)
    pallas_call x1, Pallas kernels, shards(): pl.pallas_call(kernel, out_shape=(jax.ShapeDtypeStruct((CENT, HALF), BF16...  73.9 us
    unnamed x9, local copies, waits for them, and re-layouts  5.12 us

profile of v1, /device:TPU:1, one launch (start us, length us, event | category | flops | bytes accessed | tf_op | source)
XLA Modules:
  0.0 79.7 jit_solution(14152553879215049736)
XLA Ops:
  0.6 0.0 copy-start
  0.6 1.9 %copy-done = bf16[3072,512]{1,0:T(8,128)(2,1)S(1)} copy-done((bf16[3072,512]{1,0:T(8,128)(2,1)S(1)}, bf16[3072,512]{1,0:T(8,128)(2,1)}, u32[]{:S(2)}) %copy-start) | copy-done | bytes 3145752
  2.5 0.0 copy-start.1
  2.5 0.7 copy-done.1
  3.2 0.0 copy-start.2
  3.2 0.7 copy-done.2
  3.9 73.9 %update.1 = (bf16[64,512]{1,0:T(8,128)(2,1)S(1)}, bf16[4,512]{1,0:T(4,128)(2,1)S(1)}, f32[64,512]{1,0:T(8,128)S(1)}) custom-call(bf16[3072,512]{1,0:T(8,128)(2,1)S(1)} %copy-done, s32[1,3072]{1,0:T(1,128)S(1)} %bitcast.2, s32[1,64]{1,0:T(1,128)S(1)} %bitcast.3), custom_call_target="tpu_custom_call" | custom-call | tf_op jit(solution)/shard_map/update/pallas_call | solution.py:329
  77.8 0.6 copy.9
  78.4 0.6 copy.10
  79.0 0.7 copy.11
Async XLA Ops:
  0.6 1.9 %copy-start = (bf16[3072,512]{1,0:T(8,128)(2,1)S(1)}, bf16[3072,512]{1,0:T(8,128)(2,1)}, u32[]{:S(2)}) copy-start(bf16[3072,512]{1,0:T(8,128)(2,1)} %emb_hbm.1) | copy-start | bytes 9437188
  2.5 0.7 copy-start.1
  3.2 0.7 copy-start.2

commit v2 on v1

v2 whole, which is shorter than its diff:
```python
import jax
import jax.numpy as jnp
from jax import lax
from jax.experimental import pallas as pl
from jax.experimental.pallas import tpu as pltpu
from jax.sharding import Mesh
from jax.sharding import PartitionSpec as P

NX, NY, NZ = 4, 4, 16
CENT = 64
BAND = 8
ROWS = 3072
HALF = 512
K1 = 16384
PIECES = 2
PROWS = CENT // PIECES
DP = ("dp_0", "dp_1", "dp_2")
MESH = pl.DeviceIdType.MESH
F32 = jnp.float32
BF16 = jnp.bfloat16


def dot_nt(a, b):
    return lax.dot_general(a, b, (((1,), (1,)), ((), ())), preferred_element_type=F32)


def kernel(
    emb_hbm, ids_hbm, sec_hbm,
    fc_out, sc_out, sret,
    ids_ref, sec_ref, emb, oh, part, csend, crecv, table, tables, xg, idbuf,
    asend, arecv, apart, bsend, brecv, bpart, a2send, a2recv, b2send, b2recv,
    ycsend, ycrecv, zcsend, zcrecv, zsend, zpart, zrecv, zg, gsend, yg, ssend,
    emb_sem, ids_sem, sec_sem, t_ss, t_rs, c_ss, c_rs, x_ss, x_rs, id_ss, id_rs, pt_ss, pt_rs,
    a_ss, a_rs, b_ss, b_rs, a2_ss, a2_rs, b2_ss, b2_rs,
    yc_ss, yc_rs, zc_ss, zc_rs, z_ss, z_rs, za_ss, za_rs, ya_ss, ya_rs, r_ss, r_rs,
):
    x = lax.axis_index("dp_0")
    y = lax.axis_index("dp_1")
    z = lax.axis_index("dp_2")
    c = lax.axis_index("mp")
    me = (x * NY + y) * NZ + z
    devices = NX * NY * NZ

    def chip(step):
        index = lax.rem(me + step + devices, devices)
        return (index // (NY * NZ), lax.rem(index // NZ, NY), lax.rem(index, NZ), c)

    def xdev(step, core):
        return (lax.rem(x + step, NX), y, z, core)

    def ydev(step, core):
        return (x, lax.rem(y + step, NY), z, core)

    def zdev(step):
        return (x, y, lax.rem(z + step, NZ), c)

    partner = (x, y, z, 1 - c)
    load_ids = pltpu.make_async_copy(ids_hbm, ids_ref, ids_sem)
    load_sec = pltpu.make_async_copy(sec_hbm, sec_ref, sec_sem)
    load = pltpu.make_async_copy(emb_hbm, emb, emb_sem)
    load_ids.start()
    load_sec.start()
    load.start()

    barrier = pltpu.get_barrier_semaphore()
    near = [d for k in range(1, BAND) for d in (k, -k)]
    peers = [partner] + [chip(d) for d in near]
    for step in range(1, NX):
        peers += [xdev(step, 0), xdev(step, 1)]
    for step in range(1, NY):
        peers += [ydev(step, 0), ydev(step, 1)]
    for step in range(1, NZ):
        peers.append(zdev(step))
    for peer in peers:
        pl.semaphore_signal(barrier, inc=1, device_id=peer, device_id_type=MESH)

    pending = []

    def send(src, dst, ssem, rsem, device):
        copy = pltpu.make_async_remote_copy(
            src_ref=src, dst_ref=dst, send_sem=ssem, recv_sem=rsem, device_id=device, device_id_type=MESH
        )
        copy.start()
        pending.append(copy)

    def arrived(dst, ssem, rsem):
        pltpu.make_async_remote_copy(
            src_ref=dst, dst_ref=dst, send_sem=ssem, recv_sem=rsem, device_id=partner, device_id_type=MESH
        ).wait_recv()

    load_ids.wait()
    shifted = ids_ref[...] - me * CENT
    local = jnp.where(shifted < 0, shifted + K1, shifted)
    ones_row = jnp.ones((8, 128), BF16)
    load_sec.wait()
    table[...] = jnp.zeros_like(table)
    table[0, :, pl.ds(CENT, CENT)] = sec_ref[...].astype(F32)
    idbuf[x, :, pl.ds(0, CENT)] = sec_ref[...]
    idbuf[x, :, pl.ds(CENT, CENT)] = sec_ref[...]
    for j in range(BAND):
        rows = pl.ds(j * CENT, CENT)
        wanted = lax.broadcasted_iota(jnp.int32, (CENT, ROWS), 0) + j * CENT
        oh[rows, :] = jnp.where(local == wanted, 1.0, 0.0).astype(BF16)
        folded = oh[rows, pl.ds(0, 128)]
        for k in range(1, ROWS // 128):
            folded = folded + oh[rows, pl.ds(k * 128, 128)]
        table[j, :, pl.ds(0, CENT)] = dot_nt(ones_row, folded)[0:1]

    pl.semaphore_wait(barrier, len(peers))

    for d in near:
        kept = pl.ds(d, BAND - d) if d > 0 else pl.ds(0, BAND + d)
        t = d + BAND - 1
        send(table.at[kept], tables.at[t, kept], t_ss.at[t], t_rs.at[t], chip(d))
    for step in range(1, NX):
        send(idbuf.at[x], idbuf.at[x], id_ss.at[step - 1], id_rs.at[step - 1], xdev(step, c))

    def chain_send(s):
        j = BAND - s
        for p in range(PIECES):
            rows = pl.ds(p * PROWS, PROWS)
            total = part[pl.ds(j * CENT + p * PROWS, PROWS), :]
            if s > 1:
                arrived(crecv.at[s - 2, rows], c_ss.at[s - 2, p], c_rs.at[s - 2, p])
                total = total + crecv[s - 2, rows].astype(F32)
            csend[s - 1, rows] = total.astype(BF16)
            send(csend.at[s - 1, rows], crecv.at[s - 1, rows], c_ss.at[s - 1, p], c_rs.at[s - 1, p], chip(1))

    half = BAND // 2 * CENT
    load.wait()
    part[pl.ds(half, half), :] = jnp.dot(oh[pl.ds(half, half), :], emb[...], preferred_element_type=F32)
    chain_send(1)
    part[pl.ds(0, half), :] = jnp.dot(oh[pl.ds(0, half), :], emb[...], preferred_element_type=F32)

    for step in range(1, NX):
        arrived(idbuf.at[lax.rem(x + NX - step, NX)], id_ss.at[step - 1], id_rs.at[step - 1])
    lane = lax.broadcasted_iota(jnp.int32, (1, 128), 1)
    row = lax.broadcasted_iota(jnp.int32, (NY * NZ * 8, 128), 0)
    group = x * (NY * NZ * 4) + (row // 8) * 4 + lax.rem(row, 4)
    hits = []
    for pair in range(NX // 2):
        names = jnp.where(lane < CENT, idbuf[2 * pair], idbuf[2 * pair + 1])
        hits.append(jnp.where(names == group, 1.0, 0.0))
    hit = (hits[0] + hits[1]).astype(BF16)
    for k in range(NY):
        ycsend[k] = dot_nt(ones_row, hit[k * NZ * 8 : (k + 1) * NZ * 8])[0:1]
    for step in range(1, NY):
        to = lax.rem(y + step, NY)
        send(ycsend.at[to], ycrecv.at[step - 1], yc_ss.at[step - 1], yc_rs.at[step - 1], ydev(step, c))
    chain_send(2)

    for d in near:
        kept = pl.ds(d, BAND - d) if d > 0 else pl.ds(0, BAND + d)
        t = d + BAND - 1
        arrived(tables.at[t, kept], t_ss.at[t], t_rs.at[t])
    eye = lax.broadcasted_iota(jnp.int32, (CENT, CENT), 0) == lax.broadcasted_iota(jnp.int32, (CENT, CENT), 1)
    columns, name_rows = [], []
    for j in range(BAND):
        total = table[j]
        for d in near:
            k = j + d
            if 0 <= k < BAND:
                total = total + tables[d + BAND - 1, k]
        columns.append(jnp.sum(jnp.where(eye, total[:, 0:CENT], 0.0), axis=1, keepdims=True))
        name_rows.append(table[0] if j == 0 else tables[BAND - 1 - j, 0])
    names = jnp.concatenate(
        [
            jnp.where(lane < CENT, pltpu.roll(name_rows[2 * k], CENT, 1), name_rows[2 * k + 1])
            for k in range(BAND // 2)
        ],
        axis=1,
    ).astype(jnp.int32)
    scaled = jnp.concatenate(
        [(part[pl.ds(j * CENT, CENT), :] / columns[j]).astype(BF16) for j in range(BAND)], axis=0
    )

    block = NY * NZ * 4
    quarter = NZ * 4
    fold = HALF // 2
    for step in list(range(1, NX)) + [0]:
        to = lax.rem(x + step, NX)
        wanted = lax.broadcasted_iota(jnp.int32, (block, BAND * CENT), 0) + to * block
        member = jnp.where(names == wanted, 1.0, 0.0).astype(BF16)
        sums = jnp.dot(member, scaled, preferred_element_type=F32)
        if step:
            asend[step - 1] = sums[:, :fold].astype(BF16)
            send(asend.at[step - 1], arecv.at[step - 1], a_ss.at[step - 1], a_rs.at[step - 1], xdev(step, c))
        else:
            apart[...] = sums[:, :fold]
        for k in range(NY):
            piece = sums[k * quarter : (k + 1) * quarter, fold:]
            bsend[k, to] = piece.astype(BF16)
            bpart[k, to] = piece
    for step in range(1, NY):
        to = lax.rem(y + step, NY)
        send(bsend.at[to], brecv.at[step - 1], b_ss.at[step - 1], b_rs.at[step - 1], ydev(step, c))
    chain_send(3)
    line = ycsend[y]
    for step in range(1, NY):
        arrived(ycrecv.at[step - 1], yc_ss.at[step - 1], yc_rs.at[step - 1])
        line = line + ycrecv[step - 1]
    zcsend[...] = line
    order = sorted(range(1, NZ), key=lambda step: -min(step, NZ - step))
    for step in order:
        send(zcsend, zcrecv.at[step - 1], zc_ss.at[step - 1], zc_rs.at[step - 1], zdev(step))
    chain_send(4)

    for step in range(1, NX):
        arrived(arecv.at[step - 1], a_ss.at[step - 1], a_rs.at[step - 1])
    for step in list(range(1, NY)) + [0]:
        to = lax.rem(y + step, NY)
        rows = pl.ds(pl.multiple_of(to * quarter, quarter), quarter)
        sums = apart[rows, :]
        for k in range(NX - 1):
            sums = sums + arecv[k, rows].astype(F32)
        if step:
            a2send[step - 1] = sums.astype(BF16)
            send(a2send.at[step - 1], a2recv.at[step - 1], a2_ss.at[step - 1], a2_rs.at[step - 1], ydev(step, c))
    first_half = sums
    for step in range(1, NY):
        arrived(brecv.at[step - 1], b_ss.at[step - 1], b_rs.at[step - 1])
    for step in list(range(1, NX)) + [0]:
        to = lax.rem(x + step, NX)
        sums = bpart[y, to]
        for k in range(NY - 1):
            sums = sums + brecv[k, to].astype(F32)
        if step:
            b2send[step - 1] = sums.astype(BF16)
            send(b2send.at[step - 1], b2recv.at[step - 1], b2_ss.at[step - 1], b2_rs.at[step - 1], xdev(step, c))
    second_half = sums
    chain_send(5)
    for step in range(1, NY):
        arrived(a2recv.at[step - 1], a2_ss.at[step - 1], a2_rs.at[step - 1])
        first_half = first_half + a2recv[step - 1].astype(F32)
    for step in range(1, NX):
        arrived(b2recv.at[step - 1], b2_ss.at[step - 1], b2_rs.at[step - 1])
        second_half = second_half + b2recv[step - 1].astype(F32)

    first_half = first_half.reshape(NZ // 2, 8, fold)
    second_half = second_half.reshape(NZ // 2, 8, fold)
    low = lax.broadcasted_iota(jnp.int32, (NZ // 2, 8, fold), 1) < 4
    even = jnp.where(low, first_half, pltpu.roll(second_half, 4, 1))
    odd = jnp.where(low, pltpu.roll(first_half, 4, 1), second_half)
    for k in range(NZ // 2):
        zpart[2 * k] = even[k]
        zpart[2 * k + 1] = odd[k]
    zsend[...] = zpart[...].astype(BF16)
    for step in order:
        to = lax.rem(z + step, NZ)
        send(zsend.at[to], zrecv.at[step - 1], z_ss.at[step - 1], z_rs.at[step - 1], zdev(step))
    chain_send(6)
    counts = zcsend[...]
    for step in range(1, NZ):
        arrived(zcrecv.at[step - 1], zc_ss.at[step - 1], zc_rs.at[step - 1])
        counts = counts + zcrecv[step - 1]
    eight = lax.broadcasted_iota(jnp.int32, (8, 128), 0) + z * 8 == lax.broadcasted_iota(jnp.int32, (8, 128), 1)
    second_counts = jnp.sum(jnp.where(eight, counts, 0.0), axis=1, keepdims=True)
    sums = zpart[z]
    for step in reversed(order):
        arrived(zrecv.at[step - 1], z_ss.at[step - 1], z_rs.at[step - 1])
        sums = sums + zrecv[step - 1].astype(F32)
    second = (sums / second_counts).astype(BF16)
    zg[z] = second
    for step in order:
        send(zg.at[z], zg.at[z], za_ss.at[step - 1], za_rs.at[step - 1], zdev(step))
    second32 = second.astype(F32)
    sc_out[:, pl.ds(0, fold)] = second32[0:4].astype(BF16)
    sc_out[:, pl.ds(fold, fold)] = second32[4:8].astype(BF16)
    chain_send(7)

    last = BAND - 2
    for p in range(PIECES):
        rows = pl.ds(p * PROWS, PROWS)
        arrived(crecv.at[last, rows], c_ss.at[last, p], c_rs.at[last, p])
        total = part[rows, :] + crecv[last, rows].astype(F32)
        done = (total / columns[0][p * PROWS : (p + 1) * PROWS]).astype(BF16)
        fc_out[rows, :] = done
        xg[c, x, rows] = done
        for step in range(1, NX):
            send(xg.at[c, x, rows], xg.at[c, x, rows], x_ss.at[step - 1, p], x_rs.at[step - 1, p], xdev(step, c))
    for step in range(1, NX):
        source = lax.rem(x + NX - step, NX)
        for p in range(PIECES):
            rows = pl.ds(p * PROWS, PROWS)
            arrived(xg.at[c, source, rows], x_ss.at[step - 1, p], x_rs.at[step - 1, p])
    send(xg.at[c], xg.at[c], pt_ss, pt_rs, partner)
    for step in reversed(order):
        arrived(zg.at[lax.rem(z + NZ - step, NZ)], za_ss.at[step - 1], za_rs.at[step - 1])

    gathered = zg[...].reshape(NZ * 8, fold)
    index = lax.broadcasted_iota(jnp.int32, (quarter, NZ * 8), 0)
    column = lax.broadcasted_iota(jnp.int32, (quarter, NZ * 8), 1)
    place = (index // 4) * 8 + lax.rem(index, 4)
    for h in range(2):
        pick = jnp.where(column == place + 4 * h, 1.0, 0.0).astype(BF16)
        picked = jnp.dot(pick, gathered, preferred_element_type=F32).astype(BF16)
        gsend[:, pl.ds(h * fold, fold)] = picked
    scorer = y // (NY // 2)
    slot = lax.rem(y, NY // 2)
    for step in range(1, NY):
        send(gsend, yg.at[c, slot], ya_ss.at[step], ya_rs.at[c, slot], ydev(step, scorer))
    own_scorer = scorer == c
    to_scorer = pltpu.make_async_remote_copy(
        src_ref=gsend, dst_ref=yg.at[c, slot], send_sem=ya_ss.at[0], recv_sem=ya_rs.at[c, slot],
        device_id=partner, device_id_type=MESH,
    )

    @pl.when(own_scorer)
    def _():
        yg[c, slot] = gsend[...]

    @pl.when(jnp.logical_not(own_scorer))
    def _():
        to_scorer.start()

    arrived(xg.at[1 - c], pt_ss, pt_rs)
    for s in range(NY // 2):
        for k in range(2):
            here = jnp.logical_and(c * (NY // 2) + s == y, c == k)

            @pl.when(jnp.logical_not(here))
            def _():
                arrived(yg.at[k, s], ya_ss.at[0], ya_rs.at[k, s])

    groups = NY // 2 * quarter
    scores = jnp.zeros((NX * CENT, groups), F32)
    squares = jnp.zeros((groups, 1), F32)
    for k in range(2):
        b = yg[k].reshape(groups, HALF)
        scores = scores + dot_nt(xg[k].reshape(NX * CENT, HALF), b)
        b32 = b.astype(F32)
        squares = squares + jnp.sum(b32 * b32, axis=1, keepdims=True)
    eye = lax.broadcasted_iota(jnp.int32, (groups, groups), 0) == lax.broadcasted_iota(jnp.int32, (groups, groups), 1)
    norm_row = jnp.sum(jnp.where(eye, squares, 0.0), axis=0, keepdims=True)
    ssend[...] = (scores - 0.5 * norm_row).astype(BF16).reshape(NX, CENT, groups)
    holder = x // (NX // 2)
    out_slot = lax.rem(x, NX // 2) * 2 + c
    for step in range(1, NX):
        to = lax.rem(x + step, NX)
        send(ssend.at[to], sret.at[out_slot], r_ss.at[step], r_rs.at[out_slot], xdev(step, holder))
    own_holder = holder == c
    to_holder = pltpu.make_async_remote_copy(
        src_ref=ssend.at[x], dst_ref=sret.at[out_slot], send_sem=r_ss.at[0], recv_sem=r_rs.at[out_slot],
        device_id=partner, device_id_type=MESH,
    )

    @pl.when(own_holder)
    def _():
        sret[out_slot] = ssend[x]

    @pl.when(jnp.logical_not(own_holder))
    def _():
        to_holder.start()

    for copy in pending:
        copy.wait_send()

    @pl.when(jnp.logical_not(own_scorer))
    def _():
        to_scorer.wait_send()

    @pl.when(jnp.logical_not(own_holder))
    def _():
        to_holder.wait_send()

    for s in range(NX):
        here = jnp.logical_and(c * (NX // 2) + s // 2 == x, c == s % 2)

        @pl.when(jnp.logical_not(here))
        def _():
            arrived(sret.at[s], r_ss.at[0], r_rs.at[s])


def write_out(fc, sc, sret, fc_out, sc_out, scores_out, wide, sems):
    copies = [
        pltpu.make_async_copy(fc, fc_out, sems.at[0]),
        pltpu.make_async_copy(sc, sc_out, sems.at[1]),
    ]
    for copy in copies:
        copy.start()
    groups = sret.shape[2]
    for s in range(NX):
        wide[:, pl.ds(s * groups, groups)] = sret[s].astype(F32)
    copies.append(pltpu.make_async_copy(wide, scores_out, sems.at[2]))
    copies[2].start()
    for copy in copies:
        copy.wait()


def shards(embeddings, first_level, second_level):
    dma = pltpu.SemaphoreType.DMA
    block = NY * NZ * 4
    quarter = NZ * 4
    groups = NY // 2 * quarter
    fold = HALF // 2
    vmem = pl.BlockSpec(memory_space=pltpu.VMEM)
    hbm = pl.BlockSpec(memory_space=pltpu.HBM)
    operands = (embeddings, first_level.reshape(1, ROWS), second_level.reshape(1, CENT))
    first, second, returned = pl.pallas_call(
        kernel,
        out_shape=(
            jax.ShapeDtypeStruct((CENT, HALF), BF16),
            jax.ShapeDtypeStruct((4, HALF), BF16),
            jax.ShapeDtypeStruct((NX, CENT, groups), BF16),
        ),
        in_specs=[hbm] * 3,
        out_specs=(vmem,) * 3,
        scratch_shapes=[
            pltpu.VMEM((1, ROWS), jnp.int32),
            pltpu.VMEM((1, CENT), jnp.int32),
            pltpu.VMEM((ROWS, HALF), BF16),
            pltpu.VMEM((BAND * CENT, ROWS), BF16),
            pltpu.VMEM((BAND * CENT, HALF), F32),
            pltpu.VMEM((BAND - 1, CENT, HALF), BF16),
            pltpu.VMEM((BAND - 1, CENT, HALF), BF16),
            pltpu.VMEM((BAND, 1, 128), F32),
            pltpu.VMEM((2 * BAND - 1, BAND, 1, 128), F32),
            pltpu.VMEM((2, NX, CENT, HALF), BF16),
            pltpu.VMEM((NX, 1, 128), jnp.int32),
            pltpu.VMEM((NX - 1, block, fold), BF16),
            pltpu.VMEM((NX - 1, block, fold), BF16),
            pltpu.VMEM((block, fold), F32),
            pltpu.VMEM((NY, NX, quarter, fold), BF16),
            pltpu.VMEM((NY - 1, NX, quarter, fold), BF16),
            pltpu.VMEM((NY, NX, quarter, fold), F32),
            pltpu.VMEM((NY - 1, quarter, fold), BF16),
            pltpu.VMEM((NY - 1, quarter, fold), BF16),
            pltpu.VMEM((NX - 1, quarter, fold), BF16),
            pltpu.VMEM((NX - 1, quarter, fold), BF16),
            pltpu.VMEM((NY, 1, 128), F32),
            pltpu.VMEM((NY - 1, 1, 128), F32),
            pltpu.VMEM((1, 128), F32),
            pltpu.VMEM((NZ - 1, 1, 128), F32),
            pltpu.VMEM((NZ, 8, fold), BF16),
            pltpu.VMEM((NZ, 8, fold), F32),
            pltpu.VMEM((NZ - 1, 8, fold), BF16),
            pltpu.VMEM((NZ, 8, fold), BF16),
            pltpu.VMEM((quarter, HALF), BF16),
            pltpu.VMEM((2, NY // 2, quarter, HALF), BF16),
            pltpu.VMEM((NX, CENT, groups), BF16),
            dma, dma, dma,
            dma((2 * BAND - 1,)), dma((2 * BAND - 1,)),
            dma((BAND - 1, PIECES)), dma((BAND - 1, PIECES)),
            dma((NX - 1, PIECES)), dma((NX - 1, PIECES)),
            dma((NX - 1,)), dma((NX - 1,)),
            dma, dma,
            dma((NX - 1,)), dma((NX - 1,)),
            dma((NY - 1,)), dma((NY - 1,)),
            dma((NY - 1,)), dma((NY - 1,)),
            dma((NX - 1,)), dma((NX - 1,)),
            dma((NY - 1,)), dma((NY - 1,)),
            dma((NZ - 1,)), dma((NZ - 1,)),
            dma((NZ - 1,)), dma((NZ - 1,)),
            dma((NZ - 1,)), dma((NZ - 1,)),
            dma((NY,)), dma((2, NY // 2)),
            dma((NX,)), dma((NX,)),
        ],
        compiler_params=pltpu.CompilerParams(
            collective_id=0, has_side_effects=True, vmem_limit_bytes=40 << 20
        ),
        name="update",
    )(*(pltpu.with_memory_space_constraint(a, pltpu.HBM) for a in operands))
    return pl.pallas_call(
        write_out,
        out_shape=(
            jax.ShapeDtypeStruct((CENT, HALF), BF16),
            jax.ShapeDtypeStruct((4, HALF), BF16),
            jax.ShapeDtypeStruct((CENT, HALF), F32),
        ),
        in_specs=[vmem] * 3,
        out_specs=(hbm,) * 3,
        scratch_shapes=[pltpu.VMEM((CENT, HALF), F32), dma((3,))],
        compiler_params=pltpu.CompilerParams(vmem_limit_bytes=8 << 20),
        name="write_out",
    )(first, second, returned)


def solution(mesh):
    torus = Mesh(mesh.devices.reshape(NX, NY, NZ, mesh.shape["mp"]), (*DP, "mp"))
    return jax.shard_map(
        shards,
        mesh=torus,
        in_specs=(P(DP, "mp"), P(DP), P(DP, None)),
        out_specs=(P(DP, "mp"), P(DP, "mp"), P(DP, "mp")),
        check_vma=False,
    )
```

time: 79.9 us -> 67.2 us (0.84)
  Pallas kernels: 73.9 us -> 66.4 us
  local copies, waits for them, and re-layouts: 5.12 us -> 0 us
    pallas_call x1, Pallas kernels: 73.9 us -> 65.7 us  [shards(): pl.pallas_call(kernel, out_shape=(jax.ShapeDtypeStruct((CENT, HALF), BF16...]
    unnamed x9 -> x0, local copies, waits for them, and re-layouts: 5.12 us -> none
where the time goes in v2:
time: 67.2 us; the launch traced here: 67 us
  Pallas kernels  66.4 us (99%)
    pallas_call x1, Pallas kernels, shards(): pl.pallas_call(kernel, out_shape=(jax.ShapeDtypeStruct((CENT, HALF), BF16...  65.7 us

profile of v2, /device:TPU:1, one launch (start us, length us, event | category | flops | bytes accessed | tf_op | source)
XLA Modules:
  0.0 67.0 jit_solution(15961246483988140072)
XLA Ops:
  0.6 65.7 %update.1 = (bf16[64,512]{1,0:T(8,128)(2,1)S(1)}, bf16[4,512]{1,0:T(4,128)(2,1)S(1)}, bf16[4,64,128]{2,1,0:T(8,128)(2,1)S(1)}) custom-call(bf16[3072,512]{1,0:T(8,128)(2,1)} %emb_hbm.1, s32[1,3072]{1,0:T(1,128)} %bitcast.2, s32[1,64]{1,0:T(1,128)} %bitcast.3), custom_call_target="tpu_custom_call" | custom-call | tf_op jit(solution)/shard_map/update/pallas_call | solution.py:399
  66.3 0.7 %write_out.1 = (bf16[64,512]{1,0:T(8,128)(2,1)}, bf16[4,512]{1,0:T(4,128)(2,1)}, f32[64,512]{1,0:T(8,128)}) custom-call(bf16[64,512]{1,0:T(8,128)(2,1)S(1)} %get-tuple-element.6.fc, bf16[4,512]{1,0:T(4,128)(2,1)S(1)} %get-tuple-element.7.sc, bf16[4,64,128]{2,1,0:T(8,128)(2,1)S(1)} %get-tuple-element.8.sret), custom_call_target="tpu_custom_call" | custom-call | tf_op jit(solution)/shard_map/write_out/pallas_call | solution.py:463

commit v3 on v2

v3 whole, which is shorter than its diff:
```python
import jax
import jax.numpy as jnp
from jax import lax
from jax.experimental import pallas as pl
from jax.experimental.pallas import tpu as pltpu
from jax.sharding import Mesh
from jax.sharding import PartitionSpec as P

NX, NY, NZ = 4, 4, 16
CENT = 64
BAND = 8
ROWS = 3072
HALF = 512
K1 = 16384
DP = ("dp_0", "dp_1", "dp_2")
MESH = pl.DeviceIdType.MESH
F32 = jnp.float32
BF16 = jnp.bfloat16


def dot_nt(a, b):
    return lax.dot_general(a, b, (((1,), (1,)), ((), ())), preferred_element_type=F32)


def kernel(
    emb_hbm, ids_hbm, sec_hbm,
    fc_out, sc_out, sret,
    ids_ref, sec_ref, emb, oh, part, partb, csend, crecv, table, tables, xg, idbuf,
    asend, arecv, apart, bsend, brecv, bpart, a2send, a2recv, b2send, b2recv,
    ycsend, ycrecv, zcsend, zcrecv, zsend, zpart, zrecv, zg, yg, ssend,
    emb_sem, ids_sem, sec_sem, t_ss, t_rs, c_ss, c_rs, x_ss, x_rs, id_ss, id_rs, pt_ss, pt_rs,
    a_ss, a_rs, b_ss, b_rs, a2_ss, a2_rs, b2_ss, b2_rs,
    yc_ss, yc_rs, zc_ss, zc_rs, z_ss, z_rs, za_ss, za_rs, ya_ss, ya_rs, pg_ss, r_ss, r_rs,
):
    x = lax.axis_index("dp_0")
    y = lax.axis_index("dp_1")
    z = lax.axis_index("dp_2")
    c = lax.axis_index("mp")
    me = (x * NY + y) * NZ + z
    devices = NX * NY * NZ

    def chip(step):
        index = lax.rem(me + step + devices, devices)
        return (index // (NY * NZ), lax.rem(index // NZ, NY), lax.rem(index, NZ), c)

    def xdev(step, core):
        return (lax.rem(x + step, NX), y, z, core)

    def ydev(step, core):
        return (x, lax.rem(y + step, NY), z, core)

    def zdev(step):
        return (x, y, lax.rem(z + step, NZ), c)

    partner = (x, y, z, 1 - c)
    load_ids = pltpu.make_async_copy(ids_hbm, ids_ref, ids_sem)
    load_sec = pltpu.make_async_copy(sec_hbm, sec_ref, sec_sem)
    load = pltpu.make_async_copy(emb_hbm, emb, emb_sem)
    load_ids.start()
    load_sec.start()
    load.start()

    barrier = pltpu.get_barrier_semaphore()
    near = [d for k in range(1, BAND) for d in (k, -k)]
    peers = [partner] + [chip(d) for d in near]
    for step in range(1, NX):
        peers += [xdev(step, 0), xdev(step, 1)]
    for step in range(1, NY):
        peers += [ydev(step, 0), ydev(step, 1)]
    for step in range(1, NZ):
        peers.append(zdev(step))
    for peer in peers:
        pl.semaphore_signal(barrier, inc=1, device_id=peer, device_id_type=MESH)

    pending = []

    def send(src, dst, ssem, rsem, device):
        copy = pltpu.make_async_remote_copy(
            src_ref=src, dst_ref=dst, send_sem=ssem, recv_sem=rsem, device_id=device, device_id_type=MESH
        )
        copy.start()
        pending.append(copy)

    def drain():
        while pending:
            pending.pop(0).wait_send()

    def arrived(dst, ssem, rsem):
        pltpu.make_async_remote_copy(
            src_ref=dst, dst_ref=dst, send_sem=ssem, recv_sem=rsem, device_id=partner, device_id_type=MESH
        ).wait_recv()

    load_ids.wait()
    shifted = ids_ref[...] - me * CENT
    local = jnp.where(shifted < 0, shifted + K1, shifted)
    ones_row = jnp.ones((8, 128), BF16)
    load_sec.wait()
    table[...] = jnp.zeros_like(table)
    table[0, :, pl.ds(CENT, CENT)] = sec_ref[...].astype(F32)
    idbuf[x, :, pl.ds(0, CENT)] = sec_ref[...]
    idbuf[x, :, pl.ds(CENT, CENT)] = sec_ref[...]
    for j in range(BAND):
        rows = pl.ds(j * CENT, CENT)
        wanted = lax.broadcasted_iota(jnp.int32, (CENT, ROWS), 0) + j * CENT
        oh[rows, :] = jnp.where(local == wanted, 1.0, 0.0).astype(BF16)
        folded = oh[rows, pl.ds(0, 128)]
        for k in range(1, ROWS // 128):
            folded = folded + oh[rows, pl.ds(k * 128, 128)]
        table[j, :, pl.ds(0, CENT)] = dot_nt(ones_row, folded)[0:1]

    pl.semaphore_wait(barrier, len(peers))

    for d in near:
        kept = pl.ds(d, BAND - d) if d > 0 else pl.ds(0, BAND + d)
        t = d + BAND - 1
        send(table.at[kept], tables.at[t, kept], t_ss.at[t], t_rs.at[t], chip(d))
    for step in range(1, NX):
        send(idbuf.at[x], idbuf.at[x], id_ss.at[step - 1], id_rs.at[step - 1], xdev(step, c))

    def band(j):
        return pl.ds(j * CENT, CENT)

    def step_one(q):
        send(partb.at[band(2 * q + 1)], crecv.at[q], c_ss.at[q], c_rs.at[q], chip(1))

    def joined(j):
        arrived(crecv.at[j // 2], c_ss.at[j // 2], c_rs.at[j // 2])
        return part[band(j), :] + crecv[j // 2].astype(F32)

    def step_two(j):
        k = 4 + j // 4
        csend[k - 4] = joined(j).astype(BF16)
        send(csend.at[k - 4], crecv.at[k], c_ss.at[k], c_rs.at[k], chip(2))

    def received(k):
        arrived(crecv.at[k], c_ss.at[k], c_rs.at[k])
        return crecv[k].astype(F32)

    def step_three():
        csend[2] = (joined(4) + received(5)).astype(BF16)
        send(csend.at[2], crecv.at[6], c_ss.at[6], c_rs.at[6], chip(4))

    half = BAND // 2 * CENT
    load.wait()
    for begin in (half, 0):
        rows = pl.ds(begin, half)
        sums = jnp.dot(oh[rows, :], emb[...], preferred_element_type=F32)
        part[rows, :] = sums
        partb[rows, :] = sums.astype(BF16)
        if begin:
            step_one(3)
            step_one(2)

    step_one(1)
    step_one(0)
    for step in range(1, NX):
        arrived(idbuf.at[lax.rem(x + NX - step, NX)], id_ss.at[step - 1], id_rs.at[step - 1])
    lane = lax.broadcasted_iota(jnp.int32, (1, 128), 1)
    block = NY * NZ * 4
    quarter = NZ * 4
    group = lax.broadcasted_iota(jnp.int32, (block, 128), 0) + x * block
    hits = []
    for pair in range(NX // 2):
        names = jnp.where(lane < CENT, idbuf[2 * pair], idbuf[2 * pair + 1])
        hits.append(jnp.where(names == group, 1.0, 0.0))
    hit = (hits[0] + hits[1]).astype(BF16)
    ycsend[...] = jnp.zeros_like(ycsend)
    for k in range(NY):
        ycsend[k, :, pl.ds(0, CENT)] = dot_nt(ones_row, hit[k * quarter : (k + 1) * quarter])[0:1]
    for step in range(1, NY):
        to = lax.rem(y + step, NY)
        send(ycsend.at[to], ycrecv.at[step - 1], yc_ss.at[step - 1], yc_rs.at[step - 1], ydev(step, c))
    step_two(6)

    for d in near:
        kept = pl.ds(d, BAND - d) if d > 0 else pl.ds(0, BAND + d)
        t = d + BAND - 1
        arrived(tables.at[t, kept], t_ss.at[t], t_rs.at[t])
    totals, name_rows = [], []
    for j in range(BAND):
        total = table[j]
        for d in near:
            k = j + d
            if 0 <= k < BAND:
                total = total + tables[d + BAND - 1, k]
        totals.append(total)
        name_rows.append(table[0] if j == 0 else tables[BAND - 1 - j, 0])
    names, weights = [], []
    for k in range(BAND // 2):
        names.append(jnp.where(lane < CENT, pltpu.roll(name_rows[2 * k], CENT, 1), name_rows[2 * k + 1]))
        weights.append(1.0 / jnp.where(lane < CENT, totals[2 * k], pltpu.roll(totals[2 * k + 1], CENT, 1)))
    names = jnp.concatenate(names, axis=1).astype(jnp.int32)
    weights = jnp.concatenate(weights, axis=1)

    fold = HALF // 2
    far_x = [2, 1, 3, 0]
    far_y = [2, 1, 3, 0]
    for step in far_x:
        to = lax.rem(x + step, NX)
        wanted = lax.broadcasted_iota(jnp.int32, (block, BAND * CENT), 0) + to * block
        member = jnp.where(names == wanted, weights, 0.0).astype(BF16)
        sums = jnp.dot(member, partb[...], preferred_element_type=F32)
        for k in range(NY):
            apart[step, k] = sums[k * quarter : (k + 1) * quarter, :fold]
            bpart[k, to] = sums[k * quarter : (k + 1) * quarter, fold:]
        if step:
            asend[step - 1] = sums[:, :fold].reshape(NY, quarter, fold).astype(BF16)
        for k in far_y:
            at = lax.rem(y + k, NY)
            if step:
                send(
                    asend.at[step - 1, at], arecv.at[step - 1, at],
                    a_ss.at[step - 1, k], a_rs.at[step - 1, k], xdev(step, c),
                )
            if k:
                bsend[k - 1, step] = bpart[at, to].astype(BF16)
                send(
                    bsend.at[k - 1, step], brecv.at[k - 1, to],
                    b_ss.at[k - 1, step], b_rs.at[k - 1, to], ydev(k, c),
                )
    step_two(2)
    step_three()
    line = ycsend[y]
    for step in range(1, NY):
        arrived(ycrecv.at[step - 1], yc_ss.at[step - 1], yc_rs.at[step - 1])
        line = line + ycrecv[step - 1]
    zcsend[...] = line
    order = sorted(range(1, NZ), key=lambda step: -min(step, NZ - step))
    for step in order:
        send(zcsend, zcrecv.at[step - 1], zc_ss.at[step - 1], zc_rs.at[step - 1], zdev(step))

    for t in range(NY):
        step = far_y[t]
        to = lax.rem(y + step, NY)
        sums = apart[0, to]
        for k in range(1, NX):
            arrived(arecv.at[k - 1, to], a_ss.at[k - 1, step], a_rs.at[k - 1, step])
            sums = sums + arecv[k - 1, to].astype(F32)
        if step:
            a2send[step - 1] = sums.astype(BF16)
            send(a2send.at[step - 1], a2recv.at[step - 1], a2_ss.at[step - 1], a2_rs.at[step - 1], ydev(step, c))
        else:
            first_half = sums
        step = far_x[t]
        to = lax.rem(x + step, NX)
        sums = bpart[y, to]
        for k in range(1, NY):
            arrived(brecv.at[k - 1, to], b_ss.at[k - 1, step], b_rs.at[k - 1, to])
            sums = sums + brecv[k - 1, to].astype(F32)
        if step:
            b2send[step - 1] = sums.astype(BF16)
            send(b2send.at[step - 1], b2recv.at[step - 1], b2_ss.at[step - 1], b2_rs.at[step - 1], xdev(step, c))
        else:
            second_half = sums
    for step in range(1, NY):
        arrived(a2recv.at[step - 1], a2_ss.at[step - 1], a2_rs.at[step - 1])
        first_half = first_half + a2recv[step - 1].astype(F32)
    for step in range(1, NX):
        arrived(b2recv.at[step - 1], b2_ss.at[step - 1], b2_rs.at[step - 1])
        second_half = second_half + b2recv[step - 1].astype(F32)

    for k in range(NZ // 2):
        zpart[2 * k] = first_half[8 * k : 8 * k + 8]
        zpart[2 * k + 1] = second_half[8 * k : 8 * k + 8]
    zsend[...] = zpart[...].astype(BF16)
    for step in order:
        to = lax.rem(z + step, NZ)
        send(zsend.at[to], zrecv.at[step - 1], z_ss.at[step - 1], z_rs.at[step - 1], zdev(step))

    eye = lax.broadcasted_iota(jnp.int32, (CENT, CENT), 0) == lax.broadcasted_iota(jnp.int32, (CENT, CENT), 1)
    count_column = jnp.sum(jnp.where(eye, totals[0][:, 0:CENT], 0.0), axis=1, keepdims=True)
    done = ((joined(0) + received(4) + received(6)) / count_column).astype(BF16)
    fc_out[...] = done
    xg[c, x] = done
    for step in range(1, NX):
        send(xg.at[c, x], xg.at[c, x], x_ss.at[step - 1], x_rs.at[step - 1], xdev(step, c))
    counts = zcsend[...]
    for step in range(1, NZ):
        arrived(zcrecv.at[step - 1], zc_ss.at[step - 1], zc_rs.at[step - 1])
        counts = counts + zcrecv[step - 1]
    drain()
    eight = lax.broadcasted_iota(jnp.int32, (8, 128), 0) + (z // 2) * 8 == lax.broadcasted_iota(jnp.int32, (8, 128), 1)
    second_counts = jnp.sum(jnp.where(eight, counts, 0.0), axis=1, keepdims=True)
    sums = zpart[z]
    for step in reversed(order):
        arrived(zrecv.at[step - 1], z_ss.at[step - 1], z_rs.at[step - 1])
        sums = sums + zrecv[step - 1].astype(F32)
    second = (sums / second_counts).astype(BF16)
    pair, side = z // 2, lax.rem(z, 2)
    zg[pair, side] = second
    for step in order:
        send(zg.at[pair, side], zg.at[pair, side], za_ss.at[step - 1], za_rs.at[step - 1], zdev(step))
    scorer = y // (NY // 2)
    slot = lax.rem(y, NY // 2)
    drain()
    for step in range(1, NX):
        source = lax.rem(x + NX - step, NX)
        arrived(xg.at[c, source], x_ss.at[step - 1], x_rs.at[step - 1])
    send(xg.at[c], xg.at[c], pt_ss, pt_rs, partner)
    for d in (0, 1, 7, 2, 6, 3, 5, 4):
        there = lax.rem(pair + d, NZ // 2)
        for h in range(2):
            source = 2 * there + h
            step = lax.rem(z + NZ - source, NZ)
            if d:
                arrived(zg.at[there, h], za_ss.at[0], za_rs.at[step - 1])
        if not d:
            step = lax.rem(NZ + 2 * side - 1, NZ)
            arrived(zg.at[pair, 1 - side], za_ss.at[0], za_rs.at[step - 1])
            ours = zg[pair].astype(F32)
            for h in range(2):
                rows = jnp.where(side == 0, ours[h, 0:4], ours[h, 4:8])
                sc_out[:, pl.ds(h * fold, fold)] = rows.astype(BF16)
        for k in range(1, NY):
            send(zg.at[there], yg.at[c, slot, there], ya_ss.at[k - 1, d], ya_rs.at[c, slot], ydev(k, scorer))
    own_scorer = scorer == c
    to_scorer = pltpu.make_async_remote_copy(
        src_ref=zg, dst_ref=yg.at[c, slot], send_sem=pg_ss, recv_sem=ya_rs.at[c, slot],
        device_id=partner, device_id_type=MESH,
    )

    @pl.when(own_scorer)
    def _():
        yg[c, slot] = zg[...]

    @pl.when(jnp.logical_not(own_scorer))
    def _():
        to_scorer.start()

    arrived(xg.at[1 - c], pt_ss, pt_rs)
    for s in range(NY // 2):
        for k in range(2):
            here = jnp.logical_and(c * (NY // 2) + s == y, c == k)

            @pl.when(jnp.logical_not(here))
            def _():
                arrived(yg.at[k, s], pg_ss, ya_rs.at[k, s])

    groups = NY // 2 * quarter
    scores = jnp.zeros((NX * CENT, groups), F32)
    squares = jnp.zeros((groups, 1), F32)
    for k in range(2):
        for h in range(2):
            b = yg[k, :, :, h].reshape(groups, fold)
            scores = scores + dot_nt(xg[k, :, :, pl.ds(h * fold, fold)].reshape(NX * CENT, fold), b)
            b32 = b.astype(F32)
            squares = squares + jnp.sum(b32 * b32, axis=1, keepdims=True)
    eye = lax.broadcasted_iota(jnp.int32, (groups, groups), 0) == lax.broadcasted_iota(jnp.int32, (groups, groups), 1)
    norm_row = jnp.sum(jnp.where(eye, squares, 0.0), axis=0, keepdims=True)
    ssend[...] = (scores - 0.5 * norm_row).astype(BF16).reshape(NX, CENT, groups)
    holder = x // (NX // 2)
    out_slot = lax.rem(x, NX // 2) * 2 + c
    for step in range(1, NX):
        to = lax.rem(x + step, NX)
        send(ssend.at[to], sret.at[out_slot], r_ss.at[step], r_rs.at[out_slot], xdev(step, holder))
    own_holder = holder == c
    to_holder = pltpu.make_async_remote_copy(
        src_ref=ssend.at[x], dst_ref=sret.at[out_slot], send_sem=r_ss.at[0], recv_sem=r_rs.at[out_slot],
        device_id=partner, device_id_type=MESH,
    )

    @pl.when(own_holder)
    def _():
        sret[out_slot] = ssend[x]

    @pl.when(jnp.logical_not(own_holder))
    def _():
        to_holder.start()

    drain()

    @pl.when(jnp.logical_not(own_scorer))
    def _():
        to_scorer.wait_send()

    @pl.when(jnp.logical_not(own_holder))
    def _():
        to_holder.wait_send()

    for s in range(NX):
        here = jnp.logical_and(c * (NX // 2) + s // 2 == x, c == s % 2)

        @pl.when(jnp.logical_not(here))
        def _():
            arrived(sret.at[s], r_ss.at[0], r_rs.at[s])


def write_out(fc, sc, sret, fc_out, sc_out, scores_out, wide, sems):
    copies = [
        pltpu.make_async_copy(fc, fc_out, sems.at[0]),
        pltpu.make_async_copy(sc, sc_out, sems.at[1]),
    ]
    for copy in copies:
        copy.start()
    groups = sret.shape[2]
    for s in range(NX):
        wide[:, pl.ds(s * groups, groups)] = sret[s].astype(F32)
    copies.append(pltpu.make_async_copy(wide, scores_out, sems.at[2]))
    copies[2].start()
    for copy in copies:
        copy.wait()


def shards(embeddings, first_level, second_level):
    dma = pltpu.SemaphoreType.DMA
    quarter = NZ * 4
    groups = NY // 2 * quarter
    fold = HALF // 2
    vmem = pl.BlockSpec(memory_space=pltpu.VMEM)
    hbm = pl.BlockSpec(memory_space=pltpu.HBM)
    operands = (embeddings, first_level.reshape(1, ROWS), second_level.reshape(1, CENT))
    first, second, returned = pl.pallas_call(
        kernel,
        out_shape=(
            jax.ShapeDtypeStruct((CENT, HALF), BF16),
            jax.ShapeDtypeStruct((4, HALF), BF16),
            jax.ShapeDtypeStruct((NX, CENT, groups), BF16),
        ),
        in_specs=[hbm] * 3,
        out_specs=(vmem,) * 3,
        scratch_shapes=[
            pltpu.VMEM((1, ROWS), jnp.int32),
            pltpu.VMEM((1, CENT), jnp.int32),
            pltpu.VMEM((ROWS, HALF), BF16),
            pltpu.VMEM((BAND * CENT, ROWS), BF16),
            pltpu.VMEM((BAND * CENT, HALF), F32),
            pltpu.VMEM((BAND * CENT, HALF), BF16),
            pltpu.VMEM((3, CENT, HALF), BF16),
            pltpu.VMEM((BAND - 1, CENT, HALF), BF16),
            pltpu.VMEM((BAND, 1, 128), F32),
            pltpu.VMEM((2 * BAND - 1, BAND, 1, 128), F32),
            pltpu.VMEM((2, NX, CENT, HALF), BF16),
            pltpu.VMEM((NX, 1, 128), jnp.int32),
            pltpu.VMEM((NX - 1, NY, quarter, fold), BF16),
            pltpu.VMEM((NX - 1, NY, quarter, fold), BF16),
            pltpu.VMEM((NX, NY, quarter, fold), F32),
            pltpu.VMEM((NY - 1, NX, quarter, fold), BF16),
            pltpu.VMEM((NY - 1, NX, quarter, fold), BF16),
            pltpu.VMEM((NY, NX, quarter, fold), F32),
            pltpu.VMEM((NY - 1, quarter, fold), BF16),
            pltpu.VMEM((NY - 1, quarter, fold), BF16),
            pltpu.VMEM((NX - 1, quarter, fold), BF16),
            pltpu.VMEM((NX - 1, quarter, fold), BF16),
            pltpu.VMEM((NY, 1, 128), F32),
            pltpu.VMEM((NY - 1, 1, 128), F32),
            pltpu.VMEM((1, 128), F32),
            pltpu.VMEM((NZ - 1, 1, 128), F32),
            pltpu.VMEM((NZ, 8, fold), BF16),
            pltpu.VMEM((NZ, 8, fold), F32),
            pltpu.VMEM((NZ - 1, 8, fold), BF16),
            pltpu.VMEM((NZ // 2, 2, 8, fold), BF16),
            pltpu.VMEM((2, NY // 2, NZ // 2, 2, 8, fold), BF16),
            pltpu.VMEM((NX, CENT, groups), BF16),
            dma, dma, dma,
            dma((2 * BAND - 1,)), dma((2 * BAND - 1,)),
            dma((BAND - 1,)), dma((BAND - 1,)),
            dma((NX - 1,)), dma((NX - 1,)),
            dma((NX - 1,)), dma((NX - 1,)),
            dma, dma,
            dma((NX - 1, NY)), dma((NX - 1, NY)),
            dma((NY - 1, NX)), dma((NY - 1, NX)),
            dma((NY - 1,)), dma((NY - 1,)),
            dma((NX - 1,)), dma((NX - 1,)),
            dma((NY - 1,)), dma((NY - 1,)),
            dma((NZ - 1,)), dma((NZ - 1,)),
            dma((NZ - 1,)), dma((NZ - 1,)),
            dma((NZ - 1,)), dma((NZ - 1,)),
            dma((NY - 1, NZ // 2)), dma((2, NY // 2)), dma,
            dma((NX,)), dma((NX,)),
        ],
        compiler_params=pltpu.CompilerParams(
            collective_id=0, has_side_effects=True, vmem_limit_bytes=40 << 20
        ),
        name="update",
    )(*(pltpu.with_memory_space_constraint(a, pltpu.HBM) for a in operands))
    return pl.pallas_call(
        write_out,
        out_shape=(
            jax.ShapeDtypeStruct((CENT, HALF), BF16),
            jax.ShapeDtypeStruct((4, HALF), BF16),
            jax.ShapeDtypeStruct((CENT, HALF), F32),
        ),
        in_specs=[vmem] * 3,
        out_specs=(hbm,) * 3,
        scratch_shapes=[pltpu.VMEM((CENT, HALF), F32), dma((3,))],
        compiler_params=pltpu.CompilerParams(vmem_limit_bytes=8 << 20),
        name="write_out",
    )(first, second, returned)


def solution(mesh):
    torus = Mesh(mesh.devices.reshape(NX, NY, NZ, mesh.shape["mp"]), (*DP, "mp"))
    return jax.shard_map(
        shards,
        mesh=torus,
        in_specs=(P(DP, "mp"), P(DP), P(DP, None)),
        out_specs=(P(DP, "mp"), P(DP, "mp"), P(DP, "mp")),
        check_vma=False,
    )
```

time: 67.2 us -> 65.7 us (0.978)
  Pallas kernels: 66.4 us -> 64.8 us
    pallas_call x1, Pallas kernels: 65.7 us -> 64.1 us  [shards(): pl.pallas_call(kernel, out_shape=(jax.ShapeDtypeStruct((CENT, HALF), BF16...]
where the time goes in v3:
time: 65.7 us; the launch traced here: 65.5 us
  Pallas kernels  64.8 us (99%)
    pallas_call x1, Pallas kernels, shards(): pl.pallas_call(kernel, out_shape=(jax.ShapeDtypeStruct((CENT, HALF), BF16...  64.1 us

profile of v3, /device:TPU:1, one launch (start us, length us, event | category | flops | bytes accessed | tf_op | source)
XLA Modules:
  0.0 65.5 jit_solution(14864019615024581234)
XLA Ops:
  0.6 64.1 %update.1 = (bf16[64,512]{1,0:T(8,128)(2,1)S(1)}, bf16[4,512]{1,0:T(4,128)(2,1)S(1)}, bf16[4,64,128]{2,1,0:T(8,128)(2,1)S(1)}) custom-call(bf16[3072,512]{1,0:T(8,128)(2,1)} %emb_hbm.1, s32[1,3072]{1,0:T(1,128)} %bitcast.2, s32[1,64]{1,0:T(1,128)} %bitcast.3), custom_call_target="tpu_custom_call" | custom-call | tf_op jit(solution)/shard_map/update/pallas_call | solution.py:412
  64.8 0.7 %write_out.1 = (bf16[64,512]{1,0:T(8,128)(2,1)}, bf16[4,512]{1,0:T(4,128)(2,1)}, f32[64,512]{1,0:T(8,128)}) custom-call(bf16[64,512]{1,0:T(8,128)(2,1)S(1)} %get-tuple-element.6.fc, bf16[4,512]{1,0:T(4,128)(2,1)S(1)} %get-tuple-element.7.sc, bf16[4,64,128]{2,1,0:T(8,128)(2,1)S(1)} %get-tuple-element.8.sret), custom_call_target="tpu_custom_call" | custom-call | tf_op jit(solution)/shard_map/write_out/pallas_call | solution.py:476

commit v4 on v3

--- a/solution.py
+++ b/solution.py
@@ -148,10 +148,11 @@
         part[rows, :] = sums
         partb[rows, :] = sums.astype(BF16)
         if begin:
-            step_one(3)
-            step_one(2)
-
+            pass
+
+    step_one(3)
     step_one(1)
+    step_one(2)
     step_one(0)
     for step in range(1, NX):
         arrived(idbuf.at[lax.rem(x + NX - step, NX)], id_ss.at[step - 1], id_rs.at[step - 1])
@@ -170,7 +171,6 @@
     for step in range(1, NY):
         to = lax.rem(y + step, NY)
         send(ycsend.at[to], ycrecv.at[step - 1], yc_ss.at[step - 1], yc_rs.at[step - 1], ydev(step, c))
-    step_two(6)
 
     for d in near:
         kept = pl.ds(d, BAND - d) if d > 0 else pl.ds(0, BAND + d)
@@ -218,8 +218,6 @@
                     bsend.at[k - 1, step], brecv.at[k - 1, to],
                     b_ss.at[k - 1, step], b_rs.at[k - 1, to], ydev(k, c),
                 )
-    step_two(2)
-    step_three()
     line = ycsend[y]
     for step in range(1, NY):
         arrived(ycrecv.at[step - 1], yc_ss.at[step - 1], yc_rs.at[step - 1])
@@ -228,6 +226,7 @@
     order = sorted(range(1, NZ), key=lambda step: -min(step, NZ - step))
     for step in order:
         send(zcsend, zcrecv.at[step - 1], zc_ss.at[step - 1], zc_rs.at[step - 1], zdev(step))
+    step_two(6)
 
     for t in range(NY):
         step = far_y[t]
@@ -252,6 +251,7 @@
             send(b2send.at[step - 1], b2recv.at[step - 1], b2_ss.at[step - 1], b2_rs.at[step - 1], xdev(step, c))
         else:
             second_half = sums
+    step_two(2)
     for step in range(1, NY):
         arrived(a2recv.at[step - 1], a2_ss.at[step - 1], a2_rs.at[step - 1])
         first_half = first_half + a2recv[step - 1].astype(F32)
@@ -267,13 +267,7 @@
         to = lax.rem(z + step, NZ)
         send(zsend.at[to], zrecv.at[step - 1], z_ss.at[step - 1], z_rs.at[step - 1], zdev(step))
 
-    eye = lax.broadcasted_iota(jnp.int32, (CENT, CENT), 0) == lax.broadcasted_iota(jnp.int32, (CENT, CENT), 1)
-    count_column = jnp.sum(jnp.where(eye, totals[0][:, 0:CENT], 0.0), axis=1, keepdims=True)
-    done = ((joined(0) + received(4) + received(6)) / count_column).astype(BF16)
-    fc_out[...] = done
-    xg[c, x] = done
-    for step in range(1, NX):
-        send(xg.at[c, x], xg.at[c, x], x_ss.at[step - 1], x_rs.at[step - 1], xdev(step, c))
+    step_three()
     counts = zcsend[...]
     for step in range(1, NZ):
         arrived(zcrecv.at[step - 1], zc_ss.at[step - 1], zc_rs.at[step - 1])
@@ -292,11 +286,14 @@
         send(zg.at[pair, side], zg.at[pair, side], za_ss.at[step - 1], za_rs.at[step - 1], zdev(step))
     scorer = y // (NY // 2)
     slot = lax.rem(y, NY // 2)
+    eye = lax.broadcasted_iota(jnp.int32, (CENT, CENT), 0) == lax.broadcasted_iota(jnp.int32, (CENT, CENT), 1)
+    count_column = jnp.sum(jnp.where(eye, totals[0][:, 0:CENT], 0.0), axis=1, keepdims=True)
+    done = ((joined(0) + received(4) + received(6)) / count_column).astype(BF16)
+    fc_out[...] = done
+    xg[c, x] = done
+    for step in range(1, NX):
+        send(xg.at[c, x], xg.at[c, x], x_ss.at[step - 1], x_rs.at[step - 1], xdev(step, c))
     drain()
-    for step in range(1, NX):
-        source = lax.rem(x + NX - step, NX)
-        arrived(xg.at[c, source], x_ss.at[step - 1], x_rs.at[step - 1])
-    send(xg.at[c], xg.at[c], pt_ss, pt_rs, partner)
     for d in (0, 1, 7, 2, 6, 3, 5, 4):
         there = lax.rem(pair + d, NZ // 2)
         for h in range(2):
@@ -327,6 +324,10 @@
     def _():
         to_scorer.start()
 
+    for step in range(1, NX):
+        source = lax.rem(x + NX - step, NX)
+        arrived(xg.at[c, source], x_ss.at[step - 1], x_rs.at[step - 1])
+    send(xg.at[c], xg.at[c], pt_ss, pt_rs, partner)
     arrived(xg.at[1 - c], pt_ss, pt_rs)
     for s in range(NY // 2):
         for k in range(2):

time: 65.7 us -> 64.3 us (0.979)
  Pallas kernels: 64.8 us -> 63.5 us
    pallas_call x1, Pallas kernels: 64.1 us -> 62.8 us  [shards(): pl.pallas_call(kernel, out_shape=(jax.ShapeDtypeStruct((CENT, HALF), BF16...]
where the time goes in v4:
time: 64.3 us; the launch traced here: 64.1 us
  Pallas kernels  63.5 us (99%)
    pallas_call x1, Pallas kernels, shards(): pl.pallas_call(kernel, out_shape=(jax.ShapeDtypeStruct((CENT, HALF), BF16...  62.8 us

profile of v4, /device:TPU:1, one launch (start us, length us, event | category | flops | bytes accessed | tf_op | source)
XLA Modules:
  0.0 64.1 jit_solution(15790581560634346174)
XLA Ops:
  0.6 62.8 %update.1 = (bf16[64,512]{1,0:T(8,128)(2,1)S(1)}, bf16[4,512]{1,0:T(4,128)(2,1)S(1)}, bf16[4,64,128]{2,1,0:T(8,128)(2,1)S(1)}) custom-call(bf16[3072,512]{1,0:T(8,128)(2,1)} %emb_hbm.1, s32[1,3072]{1,0:T(1,128)} %bitcast.2, s32[1,64]{1,0:T(1,128)} %bitcast.3), custom_call_target="tpu_custom_call" | custom-call | tf_op jit(solution)/shard_map/update/pallas_call | solution.py:413
  63.4 0.7 %write_out.1 = (bf16[64,512]{1,0:T(8,128)(2,1)}, bf16[4,512]{1,0:T(4,128)(2,1)}, f32[64,512]{1,0:T(8,128)}) custom-call(bf16[64,512]{1,0:T(8,128)(2,1)S(1)} %get-tuple-element.6.fc, bf16[4,512]{1,0:T(4,128)(2,1)S(1)} %get-tuple-element.7.sc, bf16[4,64,128]{2,1,0:T(8,128)(2,1)S(1)} %get-tuple-element.8.sret), custom_call_target="tpu_custom_call" | custom-call | tf_op jit(solution)/shard_map/write_out/pallas_call | solution.py:477

commit v5 on v4

--- a/solution.py
+++ b/solution.py
@@ -69,7 +69,7 @@
         peers += [ydev(step, 0), ydev(step, 1)]
     for step in range(1, NZ):
         peers.append(zdev(step))
-    for peer in peers:
+    for peer in reversed(peers):
         pl.semaphore_signal(barrier, inc=1, device_id=peer, device_id_type=MESH)
 
     pending = []
@@ -81,8 +81,8 @@
         copy.start()
         pending.append(copy)
 
-    def drain():
-        while pending:
+    def drain(kept=0):
+        while len(pending) > kept:
             pending.pop(0).wait_send()
 
     def arrived(dst, ssem, rsem):
@@ -110,7 +110,7 @@
 
     pl.semaphore_wait(barrier, len(peers))
 
-    for d in near:
+    for d in reversed(near):
         kept = pl.ds(d, BAND - d) if d > 0 else pl.ds(0, BAND + d)
         t = d + BAND - 1
         send(table.at[kept], tables.at[t, kept], t_ss.at[t], t_rs.at[t], chip(d))
@@ -147,8 +147,6 @@
         sums = jnp.dot(oh[rows, :], emb[...], preferred_element_type=F32)
         part[rows, :] = sums
         partb[rows, :] = sums.astype(BF16)
-        if begin:
-            pass
 
     step_one(3)
     step_one(1)
@@ -205,13 +203,9 @@
             bpart[k, to] = sums[k * quarter : (k + 1) * quarter, fold:]
         if step:
             asend[step - 1] = sums[:, :fold].reshape(NY, quarter, fold).astype(BF16)
+            send(asend.at[step - 1], arecv.at[step - 1], a_ss.at[step - 1, 0], a_rs.at[step - 1, 0], xdev(step, c))
         for k in far_y:
             at = lax.rem(y + k, NY)
-            if step:
-                send(
-                    asend.at[step - 1, at], arecv.at[step - 1, at],
-                    a_ss.at[step - 1, k], a_rs.at[step - 1, k], xdev(step, c),
-                )
             if k:
                 bsend[k - 1, step] = bpart[at, to].astype(BF16)
                 send(
@@ -228,12 +222,14 @@
         send(zcsend, zcrecv.at[step - 1], zc_ss.at[step - 1], zc_rs.at[step - 1], zdev(step))
     step_two(6)
 
+    old = len(pending)
     for t in range(NY):
         step = far_y[t]
         to = lax.rem(y + step, NY)
         sums = apart[0, to]
         for k in range(1, NX):
-            arrived(arecv.at[k - 1, to], a_ss.at[k - 1, step], a_rs.at[k - 1, step])
+            if not t:
+                arrived(arecv.at[k - 1], a_ss.at[k - 1, 0], a_rs.at[k - 1, 0])
             sums = sums + arecv[k - 1, to].astype(F32)
         if step:
             a2send[step - 1] = sums.astype(BF16)
@@ -272,7 +268,7 @@
     for step in range(1, NZ):
         arrived(zcrecv.at[step - 1], zc_ss.at[step - 1], zc_rs.at[step - 1])
         counts = counts + zcrecv[step - 1]
-    drain()
+    drain(len(pending) - old)
     eight = lax.broadcasted_iota(jnp.int32, (8, 128), 0) + (z // 2) * 8 == lax.broadcasted_iota(jnp.int32, (8, 128), 1)
     second_counts = jnp.sum(jnp.where(eight, counts, 0.0), axis=1, keepdims=True)
     sums = zpart[z]
@@ -293,7 +289,6 @@
     xg[c, x] = done
     for step in range(1, NX):
         send(xg.at[c, x], xg.at[c, x], x_ss.at[step - 1], x_rs.at[step - 1], xdev(step, c))
-    drain()
     for d in (0, 1, 7, 2, 6, 3, 5, 4):
         there = lax.rem(pair + d, NZ // 2)
         for h in range(2):

time: 64.3 us -> 63.9 us (level)
  no operation moved by 1% of the time
where the time goes in v5:
time: 63.9 us; the launch traced here: 63.7 us
  Pallas kernels  63 us (99%)
  between operations  0.64 us (1%)
    pallas_call x1, Pallas kernels, shards(): pl.pallas_call(kernel, out_shape=(jax.ShapeDtypeStruct((CENT, HALF), BF16...  62.3 us

profile of v5, /device:TPU:1, one launch (start us, length us, event | category | flops | bytes accessed | tf_op | source)
XLA Modules:
  0.0 63.7 jit_solution(10697216449408592290)
XLA Ops:
  0.6 62.3 %update.1 = (bf16[64,512]{1,0:T(8,128)(2,1)S(1)}, bf16[4,512]{1,0:T(4,128)(2,1)S(1)}, bf16[4,64,128]{2,1,0:T(8,128)(2,1)S(1)}) custom-call(bf16[3072,512]{1,0:T(8,128)(2,1)} %emb_hbm.1, s32[1,3072]{1,0:T(1,128)} %bitcast.2, s32[1,64]{1,0:T(1,128)} %bitcast.3), custom_call_target="tpu_custom_call" | custom-call | tf_op jit(solution)/shard_map/update/pallas_call | solution.py:408
  63.0 0.7 %write_out.1 = (bf16[64,512]{1,0:T(8,128)(2,1)}, bf16[4,512]{1,0:T(4,128)(2,1)}, f32[64,512]{1,0:T(8,128)}) custom-call(bf16[64,512]{1,0:T(8,128)(2,1)S(1)} %get-tuple-element.6.fc, bf16[4,512]{1,0:T(4,128)(2,1)S(1)} %get-tuple-element.7.sc, bf16[4,64,128]{2,1,0:T(8,128)(2,1)S(1)} %get-tuple-element.8.sret), custom_call_target="tpu_custom_call" | custom-call | tf_op jit(solution)/shard_map/write_out/pallas_call | solution.py:472
